TPU v7x, 32 devices: a whole 2x2x4 slice. The times are simulated.
32 devices in a mesh: dp: 8 (over y, x, core), mp: 4 (over z).
Axes of the slice: x: 2, y: 2, z: 4, core: 2. Of those that a mesh axis runs over, the one named last changes fastest.
Arguments:
- hidden_in: bfloat16 [2, 8192, 2048], P(None, ('dp', 'mp')), may hold values from -6 to 6
- counts: int32 [2, 8], P(None, 'dp'), may hold values from 20 to 50, as said below
- summary: float32 [50, 2048], replicated, may hold values from -6 to 6
- query_weight: bfloat16 [2048, 2048], P('dp', 'mp'), may hold values from -0.125 to 0.125
- query_bias: bfloat16 [2048], P('mp'), may hold values from -1.75 to 1.75
- key_weight: bfloat16 [2048, 2048], P('dp', 'mp'), may hold values from -0.125 to 0.125
- value_weight: bfloat16 [2048, 2048], P('dp', 'mp'), may hold values from -0.125 to 0.125
- value_bias: bfloat16 [2048], P('mp'), may hold values from -1.75 to 1.75
- out_weight: bfloat16 [2048, 2048], P('mp', 'dp'), may hold values from -2 to 2
- out_bias: bfloat16 [2048], replicated, may hold values from -1.25 to 1.25
- up_weight: bfloat16 [2048, 8192], P('dp', 'mp'), may hold values from -0.125 to 0.125
- up_bias: bfloat16 [8192], P('mp'), may hold values from -1.75 to 1.75
- down_weight: bfloat16 [8192, 2048], P('mp', 'dp'), may hold values from -0.0625 to 0.0625
- down_bias: bfloat16 [2048], replicated, may hold values from -1.25 to 1.25
- attn_gain: float32 [2048], replicated, may hold values from 0.5 to 1.5
- attn_shift: float32 [2048], replicated, may hold values from -0.625 to 0.625
- mlp_gain: float32 [2048], replicated, may hold values from 0.5 to 1.5
- mlp_shift: float32 [2048], replicated, may hold values from -0.625 to 0.625
- cotangent: bfloat16 [2, 8192, 2048], P(None, ('dp', 'mp')), may hold values from -6 to 6
Outputs:
- layer_out: bfloat16 [2, 8192, 2048], P(None, ('dp', 'mp'))
- grad_input: float32 [2, 8192, 2048], P(None, ('dp', 'mp'))
- grad_summary: float32 [50, 2048], replicated
- grad_query_weight: float32 [2048, 2048], P('dp', 'mp')
- grad_query_bias: float32 [2048], P('mp')
- grad_key_weight: float32 [2048, 2048], P('dp', 'mp')
- grad_value_weight: float32 [2048, 2048], P('dp', 'mp')
- grad_value_bias: float32 [2048], P('mp')
- grad_out_weight: float32 [2048, 2048], P('mp', 'dp')
- grad_out_bias: float32 [2048], replicated
- grad_up_weight: float32 [2048, 8192], P('dp', 'mp')
- grad_up_bias: float32 [8192], P('mp')
- grad_down_weight: float32 [8192, 2048], P('mp', 'dp')
- grad_down_bias: float32 [2048], replicated
- grad_attn_gain: float32 [2048], replicated
- grad_attn_shift: float32 [2048], replicated
- grad_mlp_gain: float32 [2048], replicated
- grad_mlp_shift: float32 [2048], replicated
Inputs may be any that keep to these rules, and one draw needn't show every extreme that they name: `counts`: an item's count c marks the first c of its 50 prefix slots and the first c of its 50 appended slots as used.
All inputs are finite; a program needn't handle non-finite values.
Results may differ from a plain program's by a relative error of at most 0.02.
Values may be sent and summed in bfloat16 or wider, within the bound.
No kernel may reach another device: no remote copies, remote signals or barrier semaphores. Data moves between devices by JAX's collectives and lax.ppermute only.
A program may use at most 256 MiB of HBM per device.

v0:
```python
import math

import jax
import jax.numpy as jnp
from jax import lax
from jax.sharding import PartitionSpec as P

D = 2048
HD = 64
SUMM = 50


precise = lax.Precision.HIGHEST
gelu_coef = math.sqrt(2.0 / math.pi)


def gelu_slope(values_in):
    inner = gelu_coef * (values_in + 0.044715 * values_in * values_in * values_in)
    tangent = jnp.tanh(inner)
    return 0.5 * (1.0 + tangent) + 0.5 * values_in * (1.0 - tangent * tangent) * gelu_coef * (
        1.0 + 3.0 * 0.044715 * values_in * values_in
    )


def layer_norm(values_in, gain_vec, shift_vec):
    centred = values_in - jnp.mean(values_in, axis=-1, keepdims=True)
    spread = jnp.mean(centred * centred, axis=-1, keepdims=True)
    scaled = lax.rsqrt(spread + 1e-05)
    unit_rows = centred * scaled
    return (unit_rows * gain_vec + shift_vec, unit_rows, scaled)


def norm_back(grad_out, unit_rows, scaled, gain_vec):
    weighted = grad_out * gain_vec
    return scaled * (
        weighted
        - jnp.mean(weighted, axis=-1, keepdims=True)
        - unit_rows * jnp.mean(weighted * unit_rows, axis=-1, keepdims=True)
    )


def dense(left_side, right_side):
    return jnp.dot(left_side, right_side, preferred_element_type=jnp.float32)


def times_t(left_side, right_side):
    return lax.dot_general(
        left_side, right_side, (((1,), (1,)), ((), ())), preferred_element_type=jnp.float32
    )


def inner_rows(left_side, right_side):
    return lax.dot_general(
        left_side, right_side, (((0,), (0,)), ((), ())), preferred_element_type=jnp.float32
    )


def live_keys(seq_len, item_count):
    positions = jnp.arange(seq_len, dtype=jnp.int32)
    slot_ids = positions - (seq_len - SUMM)
    return (
        (positions >= SUMM) & (slot_ids < 0)
        | (positions < item_count)
        | (slot_ids >= 0) & (slot_ids < item_count)
    )


def block_mask(row_begin, block_rows, key_live):
    rows_here = row_begin + jnp.arange(block_rows, dtype=jnp.int32)
    columns = jnp.arange(key_live.shape[0], dtype=jnp.int32)
    return (columns[None, :] <= rows_here[:, None]) & key_live[None, :]


def shards(
    hidden_in,
    counts,
    summary,
    query_weight,
    query_bias,
    key_weight,
    value_weight,
    value_bias,
    out_weight,
    out_bias,
    up_weight,
    up_bias,
    down_weight,
    down_bias,
    attn_gain,
    attn_shift,
    mlp_gain,
    mlp_shift,
    cotangent,
):
    micro_total = hidden_in.shape[0]
    local_rows = hidden_in.shape[1]
    seq_len = local_rows * lax.axis_size("mp")
    row_offset = lax.axis_index("mp") * local_rows
    head_cols = query_weight.shape[1]
    ff_cols = up_weight.shape[1]
    local_heads = head_cols // HD
    block_rows = 512
    block_count = seq_len // block_rows
    qk_scale = HD ** (-0.5)
    bias_query = query_bias.astype(jnp.float32)
    bias_value = value_bias.astype(jnp.float32)
    bias_up = up_bias.astype(jnp.float32)
    bias_out = out_bias.astype(jnp.float32)
    bias_down = down_bias.astype(jnp.float32)
    positions = row_offset + jnp.arange(local_rows, dtype=jnp.int32)
    picker = (
        (positions - (seq_len - SUMM))[:, None] == jnp.arange(SUMM, dtype=jnp.int32)[None, :]
    ).astype(jnp.float32)
    summary_rows = jnp.dot(picker, summary, precision=precise)
    full_shapes = (
        (D, head_cols),
        (D, head_cols),
        (D, head_cols),
        (head_cols, D),
        (D, ff_cols),
        (ff_cols, D),
    )
    full_sums = tuple((jnp.zeros(shape_pair, jnp.float32) for shape_pair in full_shapes))
    head_sums = (
        jnp.zeros((head_cols,), jnp.float32),
        jnp.zeros((head_cols,), jnp.float32),
        jnp.zeros((ff_cols,), jnp.float32),
    )
    zero_width = jnp.zeros((D,), jnp.float32)
    row_sums = (
        zero_width,
        zero_width,
        zero_width,
        zero_width,
        zero_width,
        zero_width,
        jnp.zeros((SUMM, D), jnp.float32),
    )
    outputs = []
    input_grads = []
    for micro_step in range(micro_total):
        gathered = (
            lax.all_gather(query_weight, "dp", axis=0, tiled=True),
            lax.all_gather(key_weight, "dp", axis=0, tiled=True),
            lax.all_gather(value_weight, "dp", axis=0, tiled=True),
            lax.all_gather(out_weight, "dp", axis=1, tiled=True),
            lax.all_gather(up_weight, "dp", axis=0, tiled=True),
            lax.all_gather(down_weight, "dp", axis=1, tiled=True),
        )
        query_full, key_full, value_full, out_full, up_full, down_full = gathered
        key_live = live_keys(seq_len, counts[micro_step, 0])
        joined = hidden_in[micro_step].astype(jnp.float32) + summary_rows
        normed, unit_one, scale_one = layer_norm(joined, attn_gain, attn_shift)
        shard_rows = lax.all_gather(normed.astype(jnp.bfloat16), "mp", axis=0, tiled=True)
        query_part = ((dense(shard_rows, query_full) + bias_query) * qk_scale).astype(jnp.bfloat16)
        key_part = dense(shard_rows, key_full).astype(jnp.bfloat16)
        value_part = (dense(shard_rows, value_full) + bias_value).astype(jnp.bfloat16)
        projected = jnp.concatenate((shard_rows, query_part, key_part, value_part), axis=1)
        normed_full = projected[:, :D]
        query_rows = projected[:, D : D + head_cols].reshape(seq_len, local_heads, HD)
        key_rows = projected[:, D + head_cols : D + 2 * head_cols].reshape(seq_len, local_heads, HD)
        value_rows = projected[:, D + 2 * head_cols :].reshape(seq_len, local_heads, HD)

        def forward_block(block_index):
            row_begin = block_index * block_rows
            query_block = lax.dynamic_slice_in_dim(query_rows, row_begin, block_rows, 0)
            scores = jnp.einsum(
                "qhd,khd->hqk", query_block, key_rows, preferred_element_type=jnp.float32
            )
            scores = jnp.where(block_mask(row_begin, block_rows, key_live)[None], scores, -1e30)
            row_top = jnp.max(scores, axis=-1, keepdims=True)
            exp_scores = jnp.exp(scores - row_top)
            exp_total = jnp.sum(exp_scores, axis=-1, keepdims=True)
            weights_low = (exp_scores / exp_total).astype(jnp.bfloat16)
            block_out = jnp.einsum(
                "hqk,khd->qhd", weights_low, value_rows, preferred_element_type=jnp.float32
            )
            return (
                block_out.astype(jnp.bfloat16).reshape(block_rows, head_cols),
                (row_top + jnp.log(exp_total))[..., 0],
            )

        attn_blocks, log_totals = lax.map(forward_block, jnp.arange(block_count, dtype=jnp.int32))
        attended = attn_blocks.reshape(seq_len, head_cols)
        mixed_rows = (
            joined
            + lax.psum_scatter(
                dense(attended, out_full).astype(jnp.bfloat16),
                "mp",
                scatter_dimension=0,
                tiled=True,
            ).astype(jnp.float32)
            + bias_out
        )
        normed_two, unit_two, scale_two = layer_norm(mixed_rows, mlp_gain, mlp_shift)
        expand_shard_rows = lax.all_gather(
            normed_two.astype(jnp.bfloat16), "mp", axis=0, tiled=True
        )
        up_value = dense(expand_shard_rows, up_full) + bias_up
        expanded = jnp.concatenate(
            (expand_shard_rows, jax.nn.gelu(up_value, approximate=True).astype(jnp.bfloat16)),
            axis=1,
        )
        normed_two_full = expanded[:, :D]
        active = expanded[:, D:]
        layer_rows = (
            mixed_rows
            + lax.psum_scatter(
                dense(active, down_full).astype(jnp.bfloat16), "mp", scatter_dimension=0, tiled=True
            ).astype(jnp.float32)
            + bias_down
        )
        outputs.append(layer_rows.astype(jnp.bfloat16))
        grad_rows = cotangent[micro_step]
        grad_layer = grad_rows.astype(jnp.float32)
        mlp_shard_rows = lax.all_gather(grad_rows, "mp", axis=0, tiled=True)
        mlp_up_value = dense(normed_two_full, up_full) + bias_up
        grad_active = times_t(mlp_shard_rows, down_full)
        mlp_grad_up = (grad_active * gelu_slope(mlp_up_value)).astype(jnp.bfloat16)
        spread_grads = jnp.concatenate((mlp_shard_rows, mlp_grad_up), axis=1)
        grad_full = spread_grads[:, :D]
        grad_up = spread_grads[:, D:]
        micro_down = inner_rows(active, grad_full)
        micro_up = inner_rows(normed_two_full, grad_up)
        up_bias_grad = jnp.sum(grad_up.astype(jnp.float32), axis=0)
        grad_normed_two = lax.psum_scatter(
            times_t(grad_up, up_full).astype(jnp.bfloat16), "mp", scatter_dimension=0, tiled=True
        ).astype(jnp.float32)
        grad_mixed = grad_layer + norm_back(grad_normed_two, unit_two, scale_two, mlp_gain)
        attn_shard_rows = lax.all_gather(grad_mixed.astype(jnp.bfloat16), "mp", axis=0, tiled=True)
        spread_attn = jnp.concatenate(
            (attn_shard_rows, times_t(attn_shard_rows, out_full).astype(jnp.bfloat16)), axis=1
        )
        grad_mixed_full = spread_attn[:, :D]
        grad_attended = spread_attn[:, D:].reshape(seq_len, local_heads, HD)
        micro_out = inner_rows(attended, grad_mixed_full)

        def backward_block(sums_pair, block_index):
            key_sum, value_sum = sums_pair
            row_begin = block_index * block_rows
            query_block = lax.dynamic_slice_in_dim(query_rows, row_begin, block_rows, 0)
            grad_block = lax.dynamic_slice_in_dim(grad_attended, row_begin, block_rows, 0)
            scores = jnp.einsum(
                "qhd,khd->hqk", query_block, key_rows, preferred_element_type=jnp.float32
            )
            scores = jnp.where(block_mask(row_begin, block_rows, key_live)[None], scores, -1e30)
            weights_full = jnp.exp(scores - log_totals[block_index][..., None])
            grad_weights = jnp.einsum(
                "qhd,khd->hqk", grad_block, value_rows, preferred_element_type=jnp.float32
            )
            centre = jnp.sum(weights_full * grad_weights, axis=-1, keepdims=True)
            grad_scores = (weights_full * (grad_weights - centre)).astype(jnp.bfloat16)
            grad_query_block = jnp.einsum(
                "hqk,khd->qhd", grad_scores, key_rows, preferred_element_type=jnp.float32
            )
            key_sum = key_sum + jnp.einsum(
                "hqk,qhd->khd", grad_scores, query_block, preferred_element_type=jnp.float32
            )
            value_sum = value_sum + jnp.einsum(
                "hqk,qhd->khd",
                weights_full.astype(jnp.bfloat16),
                grad_block,
                preferred_element_type=jnp.float32,
            )
            return (
                (key_sum, value_sum),
                grad_query_block.astype(jnp.bfloat16).reshape(block_rows, head_cols),
            )

        zero_heads = jnp.zeros((seq_len, local_heads, HD), jnp.float32)
        (key_sum, value_sum), query_blocks = lax.scan(
            backward_block, (zero_heads, zero_heads), jnp.arange(block_count, dtype=jnp.int32)
        )
        grad_query = query_blocks.reshape(seq_len, head_cols)
        grad_key = key_sum.astype(jnp.bfloat16).reshape(seq_len, head_cols)
        grad_value = value_sum.astype(jnp.bfloat16).reshape(seq_len, head_cols)
        micro_query = inner_rows(normed_full, grad_query) * qk_scale
        micro_key = inner_rows(normed_full, grad_key)
        micro_value = inner_rows(normed_full, grad_value)
        query_bias_grad = jnp.sum(grad_query.astype(jnp.float32), axis=0) * qk_scale
        value_bias_grad = jnp.sum(grad_value.astype(jnp.float32), axis=0)
        grad_normed = lax.psum_scatter(
            (
                times_t(grad_query, query_full) * qk_scale
                + times_t(grad_key, key_full)
                + times_t(grad_value, value_full)
            ).astype(jnp.bfloat16),
            "mp",
            scatter_dimension=0,
            tiled=True,
        ).astype(jnp.float32)
        grad_joined = grad_mixed + norm_back(grad_normed, unit_one, scale_one, attn_gain)
        input_grads.append(grad_joined)
        micro_grads = (micro_query, micro_key, micro_value, micro_out, micro_up, micro_down)
        full_sums = tuple(map(jnp.add, full_sums, micro_grads))
        head_sums = (
            head_sums[0] + query_bias_grad,
            head_sums[1] + value_bias_grad,
            head_sums[2] + up_bias_grad,
        )
        row_sums = (
            row_sums[0] + jnp.sum(grad_mixed, axis=0),
            row_sums[1] + jnp.sum(grad_layer, axis=0),
            row_sums[2] + jnp.sum(grad_normed * unit_one, axis=0),
            row_sums[3] + jnp.sum(grad_normed, axis=0),
            row_sums[4] + jnp.sum(grad_normed_two * unit_two, axis=0),
            row_sums[5] + jnp.sum(grad_normed_two, axis=0),
            row_sums[6] + jnp.dot(picker.T, grad_joined, precision=precise),
        )
    weight_total = (
        lax.psum_scatter(
            full_sums[0].astype(jnp.bfloat16), "dp", scatter_dimension=0, tiled=True
        ).astype(jnp.float32),
        lax.psum_scatter(
            full_sums[1].astype(jnp.bfloat16), "dp", scatter_dimension=0, tiled=True
        ).astype(jnp.float32),
        lax.psum_scatter(
            full_sums[2].astype(jnp.bfloat16), "dp", scatter_dimension=0, tiled=True
        ).astype(jnp.float32),
        lax.psum_scatter(
            full_sums[3].astype(jnp.bfloat16), "dp", scatter_dimension=1, tiled=True
        ).astype(jnp.float32),
        lax.psum_scatter(
            full_sums[4].astype(jnp.bfloat16), "dp", scatter_dimension=0, tiled=True
        ).astype(jnp.float32),
        lax.psum_scatter(
            full_sums[5].astype(jnp.bfloat16), "dp", scatter_dimension=1, tiled=True
        ).astype(jnp.float32),
    )
    head_total = lax.psum((head_sums[0], head_sums[1], head_sums[2]), "dp")
    row_total = lax.psum(
        (row_sums[0], row_sums[1], row_sums[2], row_sums[3], row_sums[4], row_sums[5], row_sums[6]),
        ("dp", "mp"),
    )
    return (
        jnp.stack(outputs),
        jnp.stack(input_grads),
        row_total[6],
        weight_total[0],
        head_total[0],
        weight_total[1],
        weight_total[2],
        head_total[1],
        weight_total[3],
        row_total[0],
        weight_total[4],
        head_total[2],
        weight_total[5],
        row_total[1],
        row_total[2],
        row_total[3],
        row_total[4],
        row_total[5],
    )


def solution(mesh):
    in_specs = (
        P(None, ("dp", "mp"), None),
        P(None, "dp"),
        P(),
        P("dp", "mp"),
        P("mp"),
        P("dp", "mp"),
        P("dp", "mp"),
        P("mp"),
        P("mp", "dp"),
        P(),
        P("dp", "mp"),
        P("mp"),
        P("mp", "dp"),
        P(),
        P(),
        P(),
        P(),
        P(),
        P(None, ("dp", "mp"), None),
    )
    out_specs = (
        P(None, ("dp", "mp"), None),
        P(None, ("dp", "mp"), None),
        P(),
        P("dp", "mp"),
        P("mp"),
        P("dp", "mp"),
        P("dp", "mp"),
        P("mp"),
        P("mp", "dp"),
        P(),
        P("dp", "mp"),
        P("mp"),
        P("mp", "dp"),
        P(),
        P(),
        P(),
        P(),
        P(),
    )
    return jax.shard_map(shards, mesh=mesh, in_specs=in_specs, out_specs=out_specs, check_vma=False)
```

profile of v0, /device:TPU:1, one launch (start us, length us, event | category | flops | bytes accessed | tf_op | source)
XLA Modules:
  0.0 2053.1 jit_solution(16066606750939423374)
XLA Ops:
  40.4 82.5 %all-gather.17.cloned.1.call-done = bf16[1024,2048]{1,0:T(8,128)(2,1)} async-done(((bf16[256,2048]{1,0:T(8,128)(2,1)}), bf16[1024,2048]{1,0:T(8,128)(2,1)}) %all-gather.17.cloned.1.call-update) | async-done | bytes 4194320 | tf_op jit(solution)/shard_map/all_gather | solution.py:154
  128.1 23.5 %all-gather.19.cloned.1.call-done = bf16[2048,512]{1,0:T(8,128)(2,1)} async-done(((bf16[256,512]{1,0:T(8,128)(2,1)}), bf16[2048,512]{1,0:T(8,128)(2,1)}) %all-gather.19.cloned.1.call-update) | async-done | bytes 2097168 | tf_op jit(solution)/shard_map/all_gather | solution.py:143
  156.9 24.4 %all-gather.23.cloned.1.call-done = bf16[2048,512]{1,0:T(8,128)(2,1)} async-done(((bf16[256,512]{1,0:T(8,128)(2,1)}), bf16[2048,512]{1,0:T(8,128)(2,1)}) %all-gather.23.cloned.1.call-update) | async-done | bytes 2097168 | tf_op jit(solution)/shard_map/all_gather | solution.py:145
  188.6 33.1 %while.56 = (s32[]{:T(128)}, bf16[2,512,512]{2,1,0:T(8,128)(2,1)}, f32[2,8,512]{2,1,0:T(8,128)S(1)}, s32[2]{0:T(128)S(1)}, bf16[1024,8,64]{0,2,1:T(8,128)(2,1)S(...) while((s32[]{:T(128)}, bf16[2,512,512]{2,1,0:T(8,128)(2,1)}, ...), condition=%wide.region_5.6_spmd.clone, body=%wide.region_2.5_spmd.clone.sunk | while | flops 1112807936 | bytes 62003432 | solution.py:183
  229.3 64.5 %all-gather.33.cloned.1.call-done = bf16[1024,2048]{1,0:T(8,128)(2,1)} async-done(((bf16[256,2048]{1,0:T(8,128)(2,1)}), bf16[1024,2048]{1,0:T(8,128)(2,1)}) %all-gather.33.cloned.1.call-update) | async-done | bytes 4194320 | tf_op jit(solution)/shard_map/all_gather | solution.py:154
  307.8 33.3 %while.57 = (s32[]{:T(128)}, bf16[2,512,512]{2,1,0:T(8,128)(2,1)}, f32[2,8,512]{2,1,0:T(8,128)S(1)}, s32[2]{0:T(128)S(1)}, bf16[1024,8,64]{0,2,1:T(8,128)(2,1)S(...) while((s32[]{:T(128)}, bf16[2,512,512]{2,1,0:T(8,128)(2,1)}, ...), condition=%wide.region_15.16_spmd.clone, body=%wide.region_12.15_spmd.clone.sunk | while | flops 1112807936 | bytes 62003432 | solution.py:183
  371.9 79.7 %reduce-scatter.19.cloned.1.call-done = bf16[256,2048]{1,0:T(8,128)(2,1)} async-done(((bf16[1024,2048]{1,0:T(8,128)(2,1)}), bf16[256,2048]{1,0:T(8,128)(2,1)}) %reduce-scatter.19.cloned.1.call-update) | async-done | bytes 1048592 | tf_op jit(solution)/shard_map/reduce_scatter | solution.py:187
  461.7 47.2 %all-gather.29.cloned.1.call-done = bf16[2048,2048]{1,0:T(8,128)(2,1)} async-done(((bf16[256,2048]{1,0:T(8,128)(2,1)}), bf16[2048,2048]{1,0:T(8,128)(2,1)}) %all-gather.29.cloned.1.call-update) | async-done | bytes 8388624 | tf_op jit(solution)/shard_map/all_gather | solution.py:147
  508.8 82.4 %all-gather.27.cloned.1.call-done = bf16[1024,2048]{1,0:T(8,128)(2,1)} async-done(((bf16[256,2048]{1,0:T(8,128)(2,1)}), bf16[1024,2048]{1,0:T(8,128)(2,1)}) %all-gather.27.cloned.1.call-update) | async-done | bytes 4194320 | tf_op jit(solution)/shard_map/all_gather | solution.py:196
  605.9 66.8 %all-gather.41.cloned.1.call-done = bf16[1,1024,2048]{2,1,0:T(8,128)(2,1)} async-done(((bf16[1,256,2048]{2,1,0:T(8,128)(2,1)}), bf16[1,1024,2048]{2,1,0:T(8,128)(2,1)}) %all-gather.41.cloned.1.call-update) | async-done | bytes 4194320 | tf_op jit(solution)/shard_map/all_gather | solution.py:216
  672.7 56.7 %all-gather.31.cloned.1.call-done = bf16[2048,2048]{1,0:T(8,128)(2,1)} async-done(((bf16[2048,256]{1,0:T(8,128)(2,1)}), bf16[2048,2048]{1,0:T(8,128)(2,1)}) %all-gather.31.cloned.1.call-update) | async-done | bytes 8388624 | tf_op jit(solution)/shard_map/all_gather | solution.py:148
  763.2 48.0 %all-gather.35.cloned.1.call-done = bf16[1024,2048]{1,0:T(8,128)(2,1)} async-done(((bf16[256,2048]{1,0:T(8,128)(2,1)}), bf16[1024,2048]{1,0:T(8,128)(2,1)}) %all-gather.35.cloned.1.call-update) | async-done | bytes 4194320 | tf_op jit(solution)/shard_map/all_gather | solution.py:196
  825.8 66.2 %all-gather.43.cloned.1.call-done = bf16[1,1024,2048]{2,1,0:T(8,128)(2,1)} async-done(((bf16[1,256,2048]{2,1,0:T(8,128)(2,1)}), bf16[1,1024,2048]{2,1,0:T(8,128)(2,1)}) %all-gather.43.cloned.1.call-update) | async-done | bytes 4194320 | tf_op jit(solution)/shard_map/all_gather | solution.py:216
  970.1 79.5 %reduce-scatter.27.cloned.1.call-done = bf16[256,2048]{1,0:T(8,128)(2,1)} async-done(((bf16[1024,2048]{1,0:T(8,128)(2,1)}), bf16[256,2048]{1,0:T(8,128)(2,1)}) %reduce-scatter.27.cloned.1.call-update) | async-done | bytes 1048592 | tf_op jit(solution)/shard_map/reduce_scatter | solution.py:226
  1053.8 75.2 %reduce-scatter.21.cloned.1.call-done = bf16[256,2048]{1,0:T(8,128)(2,1)} async-done(((bf16[1024,2048]{1,0:T(8,128)(2,1)}), bf16[256,2048]{1,0:T(8,128)(2,1)}) %reduce-scatter.21.cloned.1.call-update) | async-done | bytes 1048592 | tf_op jit(solution)/shard_map/reduce_scatter | solution.py:208
  1129.1 79.5 %reduce-scatter.17.cloned.1.call-done = bf16[256,2048]{1,0:T(8,128)(2,1)} async-done(((bf16[1024,2048]{1,0:T(8,128)(2,1)}), bf16[256,2048]{1,0:T(8,128)(2,1)}) %reduce-scatter.17.cloned.1.call-update) | async-done | bytes 1048592 | tf_op jit(solution)/shard_map/reduce_scatter | solution.py:208
  1306.4 122.1 %while.59 = (s32[]{:T(128)}, f32[1024,8,64]{0,2,1:T(8,128)}, f32[1024,8,64]{0,2,1:T(8,128)}, bf16[2,512,512]{1,2,0:T(8,128)(2,1)}, s32[2]{0:T(128)S(1)}, /*index...) while((s32[]{:T(128)}, f32[1024,8,64]{0,2,1:T(8,128)}, ...), condition=%wide.region_34.35_spmd.clone, body=%wide.region_32.34_spmd.clone.sunk | while | flops 2738100736 | bytes 252303984 | solution.py:271
  1438.5 122.9 %while.58 = (s32[]{:T(128)}, f32[1024,8,64]{0,2,1:T(8,128)}, f32[1024,8,64]{0,2,1:T(8,128)}, bf16[2,512,512]{1,2,0:T(8,128)(2,1)}, s32[2]{0:T(128)S(1)}, /*index...) while((s32[]{:T(128)}, f32[1024,8,64]{0,2,1:T(8,128)}, ...), condition=%wide.region_25.26_spmd.clone, body=%wide.region_23.25_spmd.clone.sunk | while | flops 2738100736 | bytes 252303984 | solution.py:271
  1667.2 35.3 %reduce-scatter.35.cloned.1.call-done = bf16[256,512]{1,0:T(8,128)(2,1)} async-done(((bf16[2048,512]{1,0:T(8,128)(2,1)}), bf16[256,512]{1,0:T(8,128)(2,1)}) %reduce-scatter.35.cloned.1.call-update) | async-done | bytes 262160 | tf_op jit(solution)/shard_map/reduce_scatter | solution.py:317
  1704.3 42.9 %reduce-scatter.37.cloned.1.call-done = bf16[512,256]{1,0:T(8,128)(2,1)} async-done(((bf16[512,2048]{1,0:T(8,128)(2,1)}), bf16[512,256]{1,0:T(8,128)(2,1)}) %reduce-scatter.37.cloned.1.call-update) | async-done | bytes 262160 | tf_op jit(solution)/shard_map/reduce_scatter | solution.py:320
  1749.0 77.2 %reduce-scatter.25.cloned.1.call-done = bf16[256,2048]{1,0:T(8,128)(2,1)} async-done(((bf16[1024,2048]{1,0:T(8,128)(2,1)}), bf16[256,2048]{1,0:T(8,128)(2,1)}) %reduce-scatter.25.cloned.1.call-update) | async-done | bytes 1048592 | tf_op jit(solution)/shard_map/reduce_scatter | solution.py:282
  1828.4 78.0 %reduce-scatter.29.cloned.1.call-done = bf16[256,2048]{1,0:T(8,128)(2,1)} async-done(((bf16[1024,2048]{1,0:T(8,128)(2,1)}), bf16[256,2048]{1,0:T(8,128)(2,1)}) %reduce-scatter.29.cloned.1.call-update) | async-done | bytes 1048592 | tf_op jit(solution)/shard_map/reduce_scatter | solution.py:282
  1916.6 41.8 %all-reduce = (f32[2048]{0:T(1024)}, f32[2048]{0:T(1024)}, f32[2048]{0:T(1024)}, f32[2048]{0:T(1024)}, f32[2048]{0:T(1024)}, /*index=5*/f32[2048]{0:T(1024)}) all-reduce(f32[2048]{0:T(1024)S(1)} %add.508, f32[2048]{0:T(1024)S(1)} %add.512, f32[2048]{0:T(1024)S(1)} %add.513, ...), channel_id=1, replica_groups=mesh['dp'=8,'mp'=4] {'dp','mp'}, use_global_device_ids=true, to_apply=%region_51.52 | all-reduce | flops 12288 | bytes 98304 | tf_op jit(solution)/shard_map/psum | solution.py:331
  1962.4 81.9 %all-reduce.4.cloned.1.call-done = f32[50,2048]{1,0:T(8,128)} async-done(((f32[50,2048]{1,0:T(8,128)}), f32[50,2048]{1,0:T(8,128)}) %all-reduce.4.cloned.1.call-update) | async-done | bytes 409616 | tf_op jit(solution)/shard_map/psum | solution.py:331
  (587 shorter events, 788.9 us)
Async XLA Ops:
  14.8 166.5 %all-gather.23.cloned.1.call-start = ((), (), s32[]{:S(2)}) async-start(), calls=%async_computation.17 | async-start | bytes 2359296 | tf_op jit(solution)/shard_map/all_gather | solution.py:145
  15.4 206.4 %all-gather.25.cloned.1.call-start = ((), (), s32[]{:S(2)}) async-start(), calls=%async_computation.18 | async-start | bytes 2359296 | tf_op jit(solution)/shard_map/all_gather | solution.py:146
  16.0 277.8 %all-gather.33.cloned.1.call-start = ((), (), s32[]{:S(2)}) async-start(), calls=%async_computation.24 | async-start | bytes 5242880 | tf_op jit(solution)/shard_map/all_gather | solution.py:154
  16.6 355.3 %reduce-scatter.15.cloned.1.call-start = ((), (), s32[]{:S(2)}) async-start(), calls=%async_computation.19 | async-start | bytes 5242880 | tf_op jit(solution)/shard_map/reduce_scatter | solution.py:187
  229.0 222.6 %reduce-scatter.19.cloned.1.call-start = ((), (), s32[]{:S(2)}) async-start(), calls=%async_computation.25 | async-start | bytes 5242880 | tf_op jit(solution)/shard_map/reduce_scatter | solution.py:187
  348.3 160.6 %all-gather.29.cloned.1.call-start = ((), (), s32[]{:S(2)}) async-start(), calls=%async_computation.21 | async-start | bytes 9437184 | tf_op jit(solution)/shard_map/all_gather | solution.py:147
  349.0 242.2 %all-gather.27.cloned.1.call-start = ((), (), s32[]{:S(2)}) async-start(), calls=%async_computation.20 | async-start | bytes 5242880 | tf_op jit(solution)/shard_map/all_gather | solution.py:196
  457.4 215.3 %all-gather.41.cloned.1.call-start = ((), (), s32[]{:S(2)}) async-start(), calls=%async_computation.41 | async-start | bytes 5242880 | tf_op jit(solution)/shard_map/all_gather | solution.py:216
  459.7 269.6 %all-gather.31.cloned.1.call-start = ((), (), s32[]{:S(2)}) async-start(), calls=%async_computation.22 | async-start | bytes 9437184 | tf_op jit(solution)/shard_map/all_gather | solution.py:148
  460.3 351.0 %all-gather.35.cloned.1.call-start = ((), (), s32[]{:S(2)}) async-start(), calls=%async_computation.26 | async-start | bytes 5242880 | tf_op jit(solution)/shard_map/all_gather | solution.py:196
  461.0 431.0 %all-gather.43.cloned.1.call-start = ((), (), s32[]{:S(2)}) async-start(), calls=%async_computation.42 | async-start | bytes 5242880 | tf_op jit(solution)/shard_map/all_gather | solution.py:216
  461.6 508.5 %reduce-scatter.23.cloned.1.call-start = ((), (), s32[]{:S(2)}) async-start(), calls=%async_computation.28 | async-start | bytes 5242880 | tf_op jit(solution)/shard_map/reduce_scatter | solution.py:226
  763.2 286.4 %reduce-scatter.27.cloned.1.call-start = ((), (), s32[]{:S(2)}) async-start(), calls=%async_computation.31 | async-start | bytes 5242880 | tf_op jit(solution)/shard_map/reduce_scatter | solution.py:226
  926.2 202.9 %reduce-scatter.21.cloned.1.call-start = ((), (), s32[]{:S(2)}) async-start(), calls=%async_computation.27 | async-start | bytes 5242880 | tf_op jit(solution)/shard_map/reduce_scatter | solution.py:208
  942.4 266.2 %reduce-scatter.17.cloned.1.call-start = ((), (), s32[]{:S(2)}) async-start(), calls=%async_computation.23 | async-start | bytes 5242880 | tf_op jit(solution)/shard_map/reduce_scatter | solution.py:208
  958.7 340.3 %all-gather.39.cloned.1.call-start = ((), (), s32[]{:S(2)}) async-start(), calls=%async_computation.32 | async-start | bytes 5242880 | tf_op jit(solution)/shard_map/all_gather | solution.py:230
  1217.6 213.4 %all-gather.37.cloned.1.call-start = ((), (), s32[]{:S(2)}) async-start(), calls=%async_computation.29 | async-start | bytes 5242880 | tf_op jit(solution)/shard_map/all_gather | solution.py:230
  1218.8 413.9 %reduce-scatter.39.cloned.1.call-start = ((), (), s32[]{:S(2)}) async-start(), calls=%async_computation.39 | async-start | bytes 9437184 | tf_op jit(solution)/shard_map/reduce_scatter | solution.py:323
  1249.1 386.4 %reduce-scatter.41.cloned.1.call-start = ((), (), s32[]{:S(2)}) async-start(), calls=%async_computation.40 | async-start | bytes 9437184 | tf_op jit(solution)/shard_map/reduce_scatter | solution.py:326
  1288.4 375.1 %reduce-scatter.31.cloned.1.call-start = ((), (), s32[]{:S(2)}) async-start(), calls=%async_computation.35 | async-start | bytes 2359296 | tf_op jit(solution)/shard_map/reduce_scatter | solution.py:311
  1593.3 153.9 %reduce-scatter.37.cloned.1.call-start = ((), (), s32[]{:S(2)}) async-start(), calls=%async_computation.38 | async-start | bytes 2359296 | tf_op jit(solution)/shard_map/reduce_scatter | solution.py:320
  1601.9 224.3 %reduce-scatter.25.cloned.1.call-start = ((), (), s32[]{:S(2)}) async-start(), calls=%async_computation.30 | async-start | bytes 5242880 | tf_op jit(solution)/shard_map/reduce_scatter | solution.py:282
  1614.4 292.1 %reduce-scatter.29.cloned.1.call-start = ((), (), s32[]{:S(2)}) async-start(), calls=%async_computation.33 | async-start | bytes 5242880 | tf_op jit(solution)/shard_map/reduce_scatter | solution.py:282
  1627.5 416.8 %all-reduce.4.cloned.1.call-start = ((), (), s32[]{:S(2)}) async-start(), calls=%async_computation.34 | async-start | bytes 917504 | tf_op jit(solution)/shard_map/psum | solution.py:331
  (157 other events, 3880.3 us)
Sparse Core Ops, SparseCore 0:
  42.5 80.3 all-gather.16
  213.3 80.4 all-gather.32
  296.6 75.2 reduce-scatter.14
  374.3 77.2 reduce-scatter.18
  453.5 55.2 all-gather.28
  510.8 80.3 all-gather.26
  593.3 79.2 all-gather.40
  674.4 54.8 all-gather.30
  730.9 80.3 all-gather.34
  812.7 79.2 all-gather.42
  894.8 75.3 reduce-scatter.22
  972.4 77.2 reduce-scatter.26
  1051.8 77.2 reduce-scatter.20
  1131.3 77.2 reduce-scatter.16
  1217.7 81.2 all-gather.38
  1300.4 79.2 all-gather.36
  1383.2 69.7 reduce-scatter.38
  1456.9 71.2 reduce-scatter.40
  1616.6 41.3 reduce-scatter.32
  1661.3 41.1 reduce-scatter.34
  1706.0 41.2 reduce-scatter.36
  1749.4 76.7 reduce-scatter.24
  1829.2 77.2 reduce-scatter.28
  1916.7 127.5 all-reduce.3
  (5 shorter events, 154.0 us)
where the time goes:
time: 2060 us; the launch traced here: 2050 us
  waiting for transfers between devices  1260 us (61%)
  matrix products  513 us (25%)
  other arithmetic  122 us (6%)
  blocking collectives  64 us (3%)
  local copies, waits for them, and re-layouts  56.1 us (3%)
    reduce_scatter x2, waiting for transfers between devices, shards(): lax.psum_scatter((times_t(grad_query, query_full) * qk_scale + times_t(gr...  155 us
    reduce_scatter x2, waiting for transfers between devices, shards(): lax.psum_scatter(dense(active, down_full).astype(jnp.bfloat16), 'mp', sca...  155 us
    all_gather x2, waiting for transfers between devices, shards(): lax.all_gather(normed.astype(jnp.bfloat16), 'mp', axis=0, tiled=True)  147 us
    all_gather x2, waiting for transfers between devices, shards(): mlp_shard_rows = lax.all_gather(grad_rows, 'mp', axis=0, tiled=True)  133 us
    all_gather x2, waiting for transfers between devices, shards(): lax.all_gather(normed_two.astype(jnp.bfloat16), 'mp', axis=0, tiled=True)  130 us
    dot_general x12, matrix products, dense(): return jnp.dot(left_side, right_side, preferred_element_type=jnp.float32)  105 us
    reduce_scatter x2, waiting for transfers between devices, shards(): lax.psum_scatter(dense(attended, out_full).astype(jnp.bfloat16), 'mp', sc...  103 us
    dot_general x12, matrix products, times_t(): lax.dot_general(left_side, right_side, (((1,), (1,)), ((), ())), preferre...  101 us
  transfers between devices with their start and end apart: 29, of which 23 were waited for; matrix products, arithmetic and copies ran while one was open for 31% of the time, Pallas kernels for 0%

commit v1 on v0

v1 whole, which is shorter than its diff:
```python
import functools
import math

import jax
import jax.numpy as jnp
from jax import lax
from jax.experimental import pallas as pl
from jax.experimental.pallas import tpu as pltpu
from jax.sharding import Mesh
from jax.sharding import PartitionSpec as P

D = 2048
HD = 64
SUMM = 50

precise = lax.Precision.HIGHEST
gelu_coef = math.sqrt(2.0 / math.pi)
bf16 = jnp.bfloat16
f32 = jnp.float32
DP = ("xy", "c")
MP = ("g", "r")
ALL = ("xy", "c", "g", "r")


def gelu_pair(v):
    inner = gelu_coef * (v + 0.044715 * v * v * v)
    tangent = jnp.tanh(inner)
    half = 0.5 * (1.0 + tangent)
    slope = half + 0.5 * v * (1.0 - tangent * tangent) * gelu_coef * (1.0 + 3.0 * 0.044715 * v * v)
    return v * half, slope


def layer_norm(values_in, gain_vec, shift_vec):
    centred = values_in - jnp.mean(values_in, axis=-1, keepdims=True)
    spread = jnp.mean(centred * centred, axis=-1, keepdims=True)
    scaled = lax.rsqrt(spread + 1e-05)
    unit_rows = centred * scaled
    return (unit_rows * gain_vec + shift_vec, unit_rows, scaled)


def norm_back(grad_out, unit_rows, scaled, gain_vec):
    weighted = grad_out * gain_vec
    return scaled * (
        weighted
        - jnp.mean(weighted, axis=-1, keepdims=True)
        - unit_rows * jnp.mean(weighted * unit_rows, axis=-1, keepdims=True)
    )


def dense(left_side, right_side):
    return jnp.dot(left_side, right_side, preferred_element_type=f32)


def times_t(left_side, right_side):
    return lax.dot_general(left_side, right_side, (((1,), (1,)), ((), ())), preferred_element_type=f32)


def inner_rows(left_side, right_side):
    return lax.dot_general(left_side, right_side, (((0,), (0,)), ((), ())), preferred_element_type=f32)


def live_keys(positions, seq_len, item_count):
    slot_ids = positions - (seq_len - SUMM)
    return (
        (positions >= SUMM) & (slot_ids < 0)
        | (positions >= 0) & (positions < item_count)
        | (slot_ids >= 0) & (slot_ids < item_count)
    )


def swap_pair(values):
    return lax.ppermute(values, "r", [(0, 1), (1, 0)])


def swap_core(values):
    return lax.ppermute(values, "c", [(0, 1), (1, 0)])


def shift_up(values, step):
    size = lax.axis_size("g")
    return lax.ppermute(values, "g", [(i, i + step) for i in range(size - step)])


def shift_down(values, step):
    size = lax.axis_size("g")
    return lax.ppermute(values, "g", [(i + step, i) for i in range(size - step)])


def turn_up(values, step):
    size = lax.axis_size("g")
    return lax.ppermute(values, "g", [(i, (i + step) % size) for i in range(size)])


def turn_down(values, step):
    size = lax.axis_size("g")
    return lax.ppermute(values, "g", [((i + step) % size, i) for i in range(size)])


def cost(work, size):
    return pl.CostEstimate(flops=int(1 * work), bytes_accessed=int(1 * size), transcendentals=0)


def after(values, *earlier):
    return lax.optimization_barrier((values, earlier))[0]


def ring_order():
    size = lax.axis_size("xy")
    return list(range(size // 2)) + list(range(size - 1, size // 2 - 1, -1))


def ring_step(values, way):
    order = ring_order()
    size = len(order)
    return lax.ppermute(values, "xy", [(order[i], order[(i + way) % size]) for i in range(size)])


def ring_blocks():
    order = ring_order()
    size = len(order)
    here = jnp.asarray([order.index(i) for i in range(size)], jnp.int32)[lax.axis_index("xy")]
    offsets = [0] + [way * step for step in range(1, size // 2) for way in (-1, 1)] + [size // 2]
    chips = jnp.asarray(order, jnp.int32)[(here + jnp.asarray(offsets, jnp.int32)) % size]
    core = lax.axis_index("c")
    return jnp.concatenate((2 * chips + core, 2 * chips + 1 - core))


class RingGather:
    def __init__(self, shard):
        self.blocks = [shard]
        self.right, self.left = ring_step(shard, 1), ring_step(shard, -1)
        self.steps = lax.axis_size("xy") // 2 - 1

    def advance(self, turn):
        while self.steps > 1:
            self.blocks += [self.right, self.left]
            self.right, self.left = ring_step(self.right, 1), ring_step(self.left, -1)
            self.steps -= 1
        self.blocks += [self.right, self.left]
        half = self.right.shape[0] // 2
        right, left = turn(lambda right, left: (right[:half], left[half:]), self.right, self.left)
        self.right, self.left = ring_step(right, 1), ring_step(left, -1)

    def across(self, turn):
        self.mine = turn(lambda *parts: jnp.concatenate(parts), *self.blocks, self.right, self.left)
        self.other = swap_core(self.mine)

    def finish(self, turn):
        return turn(lambda mine, other: jnp.concatenate((mine, other)), self.mine, self.other)


class RingScatter:
    def __init__(self, total, depth):
        self.steps = lax.axis_size("xy") // 2
        self.half = depth // 2
        self.blocks = [total[i * depth : (i + 1) * depth] for i in range(2 * self.steps)]
        self.first = True
        self.send(self.blocks[-1][: self.half], self.blocks[-1][self.half :])

    def send(self, right, left):
        self.steps -= 1
        self.came = (ring_step(right, 1), ring_step(left, -1))

    def add(self, right_block, left_block, right, left):
        def total(block, part):
            return (block.astype(f32) + part.astype(f32)).astype(bf16)

        if not self.first:
            return total(right_block, right), total(left_block, left)
        half = self.half
        return (
            jnp.concatenate((total(right_block[:half], right), right_block[half:])),
            jnp.concatenate((left_block[:half], total(left_block[half:], left))),
        )

    def advance(self, turn):
        right, left = self.blocks[2 * self.steps], self.blocks[2 * self.steps - 1]
        right, left = turn(self.add, right, left, *self.came)
        self.first = False
        self.send(right, left)

    def finish(self, turn):
        while self.steps > 0:
            self.advance(turn)

        def total(block, right, left):
            return (block.astype(f32) + right.astype(f32) + left.astype(f32)).astype(bf16)

        return turn(total, self.blocks[0], *self.came)


def move_block(order_ref, in_ref, out_ref):
    out_ref[...] = in_ref[...]


def pick_columns(values, order):
    rows, columns = values.shape
    width = columns // order.shape[0]
    return pl.pallas_call(
        move_block,
        grid_spec=pltpu.PrefetchScalarGridSpec(
            num_scalar_prefetch=1,
            grid=(order.shape[0],),
            in_specs=[pl.BlockSpec((rows, width), lambda j, order_ref: (0, order_ref[j]))],
            out_specs=pl.BlockSpec((rows, width), lambda j, order_ref: (0, j)),
        ),
        out_shape=jax.ShapeDtypeStruct(values.shape, values.dtype),
        cost_estimate=cost(0, 4 * values.size * values.dtype.itemsize),
        name="pick_columns",
    )(order, values)


class SumAll:
    def __init__(self, values, turn):
        half = values.shape[0] // 2
        core = lax.axis_index("c")
        self.total, other = turn(
            lambda values: (
                lax.dynamic_slice_in_dim(values, core * half, half, 0),
                lax.dynamic_slice_in_dim(values, (1 - core) * half, half, 0),
            ),
            values,
        )
        self.came = swap_core(other)
        self.ways = []
        for axis in ("xy", "r", "g"):
            size = lax.axis_size(axis)
            bit = 1
            while bit < size:
                self.ways.append((axis, [(i, i ^ bit) for i in range(size)]))
                bit *= 2
        self.left = len(self.ways)

    def advance(self, turn):
        self.total = turn(jnp.add, self.total, self.came)
        axis, pairs = self.ways[len(self.ways) - self.left]
        self.came = lax.ppermute(self.total, axis, pairs)
        self.left -= 1

    def finish(self, turn):
        while self.left > 0:
            self.advance(turn)
        self.total = turn(jnp.add, self.total, self.came)
        other = swap_core(self.total)
        low = lax.axis_index("c") == 0
        return turn(
            lambda total, other: jnp.where(
                low, jnp.concatenate((total, other)), jnp.concatenate((other, total))
            ),
            self.total,
            other,
        )


def contract(left, right, dims):
    return lax.dot_general(left, right, (dims, ((), ())), preferred_element_type=f32)


def head_parts(near_ref, far_ref, h):
    query = near_ref[:, h * HD : (h + 1) * HD]
    key = jnp.concatenate((near_ref[:, (2 + h) * HD : (3 + h) * HD], far_ref[:, (2 + h) * HD : (3 + h) * HD]))
    value = jnp.concatenate((near_ref[:, (4 + h) * HD : (5 + h) * HD], far_ref[:, (4 + h) * HD : (5 + h) * HD]))
    return query, key, value


def attend_kernel(row_ref, key_ref, near_ref, far_ref, out_ref, log_ref):
    allowed = key_ref[...] <= row_ref[...]
    outs = []
    for h in range(2):
        query, key, value = head_parts(near_ref, far_ref, h)
        scores = jnp.where(allowed, contract(key, query, ((1,), (1,))), -1e30)
        top = jnp.max(scores, axis=0, keepdims=True)
        powers = jnp.exp(scores - top)
        whole = jnp.sum(powers, axis=0, keepdims=True)
        outs.append(contract(value, powers.astype(bf16), ((0,), (0,))) / whole)
        log_ref[0, h : h + 1, :] = top + jnp.log(whole)
    out_ref[...] = jnp.concatenate(outs, axis=0).T.astype(bf16)


def attend(near, far, row_at, key_mark):
    rows = row_at.shape[0]
    keys = rows + far.shape[0]
    pairs = near.shape[1] // (6 * HD)
    return pl.pallas_call(
        attend_kernel,
        grid=(pairs,),
        in_specs=[
            pl.BlockSpec((1, rows), lambda j: (0, 0)),
            pl.BlockSpec((keys, 1), lambda j: (0, 0)),
            pl.BlockSpec((rows, 6 * HD), lambda j: (0, j)),
            pl.BlockSpec((keys - rows, 6 * HD), lambda j: (0, j)),
        ],
        out_specs=[
            pl.BlockSpec((rows, 2 * HD), lambda j: (0, j)),
            pl.BlockSpec((1, 2, rows), lambda j: (j, 0, 0)),
        ],
        out_shape=[
            jax.ShapeDtypeStruct((rows, pairs * 2 * HD), bf16),
            jax.ShapeDtypeStruct((pairs, 2, rows), f32),
        ],
        compiler_params=pltpu.CompilerParams(vmem_limit_bytes=48 << 20),
        cost_estimate=cost(pairs * rows * keys * 8 * HD * 8, pairs * (keys + rows) * 12 * HD),
        name="attend",
    )(row_at.reshape(1, -1), key_mark, near, far)


def attend_back_kernel(row_ref, key_ref, near_ref, far_ref, grad_ref, log_ref, *rest):
    out_ref = rest[-1]
    rows = grad_ref.shape[0]
    allowed = key_ref[...] <= row_ref[...]
    grad_query, grad_key, grad_value = [], [], []
    for h in range(2):
        query, key, value = head_parts(near_ref, far_ref, h)
        grad = grad_ref[:, h * HD : (h + 1) * HD]
        scores = contract(key, query, ((1,), (1,)))
        probs = jnp.where(allowed, jnp.exp(scores - log_ref[0, h : h + 1, :]), 0.0)
        grad_probs = contract(value, grad, ((1,), (1,)))
        centre = jnp.sum(probs * grad_probs, axis=0, keepdims=True)
        grad_scores = (probs * (grad_probs - centre)).astype(bf16)
        grad_query.append(contract(key, grad_scores, ((0,), (0,))))
        grad_key.append(contract(grad_scores, query, ((1,), (0,))).astype(bf16))
        grad_value.append(contract(probs.astype(bf16), grad, ((1,), (0,))).astype(bf16))
    turned = jnp.concatenate(grad_query, axis=0).T.astype(bf16)
    out_ref[:rows, : 2 * HD] = (turned.astype(f32) * HD ** (-0.5)).astype(bf16)
    out_ref[rows:, : 2 * HD] = jnp.zeros((out_ref.shape[0] - rows, 2 * HD), bf16)
    out_ref[:, 2 * HD : 4 * HD] = jnp.concatenate(grad_key, axis=1)
    out_ref[:, 4 * HD :] = jnp.concatenate(grad_value, axis=1)


def attend_back(near, far, grad, logs, row_at, key_mark, held, part, step, steps, parts):
    rows = row_at.shape[0]
    keys = rows + far.shape[0]
    columns = near.shape[1]
    pairs = columns // (6 * HD)
    out_shape = jax.ShapeDtypeStruct((steps * keys, parts * columns), bf16)
    in_specs = [
        pl.BlockSpec((1, rows), lambda j: (0, 0)),
        pl.BlockSpec((keys, 1), lambda j: (0, 0)),
        pl.BlockSpec((rows, 6 * HD), lambda j: (0, j)),
        pl.BlockSpec((keys - rows, 6 * HD), lambda j: (0, j)),
        pl.BlockSpec((rows, 2 * HD), lambda j: (0, j)),
        pl.BlockSpec((1, 2, rows), lambda j: (j, 0, 0)),
    ]
    args = [row_at.reshape(1, -1), key_mark, near, far, grad, logs]
    if held is not None:
        in_specs.append(pl.BlockSpec(memory_space=pl.ANY))
        args.append(held)
    return pl.pallas_call(
        attend_back_kernel,
        grid=(pairs,),
        in_specs=in_specs,
        out_specs=pl.BlockSpec((keys, 6 * HD), lambda j: (step, j + part * pairs)),
        out_shape=out_shape,
        input_output_aliases={} if held is None else {6: 0},
        compiler_params=pltpu.CompilerParams(vmem_limit_bytes=48 << 20),
        cost_estimate=cost(pairs * rows * keys * 16 * HD * 8, pairs * (keys + rows) * 24 * HD),
        name="attend_back",
    )(*args)


def expand_kernel(two_ref, cot_ref, up_ref, down_ref, bias_ref, *rest):
    active_ref, grad_ref, sum_ref = rest[-3:]
    active, slope = gelu_pair(
        contract(two_ref[...], up_ref[...], ((1,), (0,))) + bias_ref[...]
    )
    active_ref[...] = active.astype(bf16)
    grad_up = (contract(cot_ref[...], down_ref[...], ((1,), (0,))) * slope).astype(bf16)
    grad_ref[...] = grad_up
    sum_ref[...] = jnp.sum(grad_up.astype(f32), axis=0, keepdims=True)


def expand(two, cot, up, down, bias, held, part, step, steps, parts):
    rows, width = two.shape
    columns = up.shape[1]
    block = min(512, columns)
    count = columns // block
    in_specs = [
        pl.BlockSpec((rows, width), lambda j: (0, 0)),
        pl.BlockSpec((rows, width), lambda j: (0, 0)),
        pl.BlockSpec((width, block), lambda j: (0, j)),
        pl.BlockSpec((width, block), lambda j: (0, j)),
        pl.BlockSpec((1, block), lambda j: (0, j)),
    ]
    args = [two, cot, up, down, bias.reshape(1, -1)]
    if held is not None:
        in_specs += [pl.BlockSpec(memory_space=pl.ANY)] * 2
        args += list(held)
    whole = jax.ShapeDtypeStruct((steps * rows, parts * columns), bf16)
    return pl.pallas_call(
        expand_kernel,
        grid=(count,),
        in_specs=in_specs,
        out_specs=[
            pl.BlockSpec((rows, block), lambda j: (step, j + part * count)),
            pl.BlockSpec((rows, block), lambda j: (step, j + part * count)),
            pl.BlockSpec((1, block), lambda j: (0, j)),
        ],
        out_shape=[whole, whole, jax.ShapeDtypeStruct((1, columns), f32)],
        input_output_aliases={} if held is None else {5: 0, 6: 1},
        compiler_params=pltpu.CompilerParams(vmem_limit_bytes=48 << 20),
        cost_estimate=cost(4 * rows * width * columns, 4 * width * columns),
        name="expand",
    )(*args)


def times_kernel(a_ref, w_ref, bias_ref, scale_ref, out_ref):
    total = contract(a_ref[...], w_ref[...], ((1,), (0,)))
    out_ref[...] = ((total + bias_ref[...]) * scale_ref[...]).astype(bf16)


def times(rows_in, weight, first, columns, bias, scale):
    rows, width = rows_in.shape
    block = math.gcd(512, columns)
    start = first // block
    return pl.pallas_call(
        times_kernel,
        grid=(columns // block,),
        in_specs=[
            pl.BlockSpec((rows, width), lambda j: (0, 0)),
            pl.BlockSpec((width, block), lambda j: (0, start + j)),
            pl.BlockSpec((1, block), lambda j: (0, j)),
            pl.BlockSpec((1, block), lambda j: (0, j)),
        ],
        out_specs=pl.BlockSpec((rows, block), lambda j: (0, j)),
        out_shape=jax.ShapeDtypeStruct((rows, columns), bf16),
        compiler_params=pltpu.CompilerParams(vmem_limit_bytes=48 << 20),
        cost_estimate=cost(2 * rows * width * columns, 2 * width * columns),
        name="times",
    )(rows_in, weight, bias.reshape(1, -1), scale.reshape(1, -1))


def back_kernel(count, rows, *refs):
    mine_ref, other_ref = refs[2 * count :]
    total = contract(refs[0][...], refs[1][...], ((1,), (1,)))
    for i in range(1, count):
        total = total + contract(refs[2 * i][...], refs[2 * i + 1][...], ((1,), (1,)))
    for i in range(mine_ref.shape[0] // rows):
        mine_ref[i * rows : (i + 1) * rows, :] = total[2 * i * rows : (2 * i + 1) * rows]
        other_ref[i * rows : (i + 1) * rows, :] = total[(2 * i + 1) * rows : (2 * i + 2) * rows].astype(bf16)


def times_back(parts, rows, sets, depth, step):
    width = parts[0][2].shape[0]
    block = min(512, width)
    in_specs, args = [], []
    for left, left_block, weight, weight_block in parts:
        in_specs.append(pl.BlockSpec((2 * sets * rows, depth), lambda j, b=left_block: (step, b)))
        in_specs.append(pl.BlockSpec((block, depth), lambda j, b=weight_block: (j, b)))
        args += [left, weight]
    out_spec = pl.BlockSpec((sets * rows, block), lambda j: (0, j))
    return pl.pallas_call(
        functools.partial(back_kernel, len(parts), rows),
        grid=(width // block,),
        in_specs=in_specs,
        out_specs=[out_spec, out_spec],
        out_shape=[
            jax.ShapeDtypeStruct((sets * rows, width), f32),
            jax.ShapeDtypeStruct((sets * rows, width), bf16),
        ],
        compiler_params=pltpu.CompilerParams(vmem_limit_bytes=56 << 20),
        cost_estimate=cost(
            4 * sets * rows * depth * width * len(parts), 2 * depth * width * len(parts)
        ),
        name="times_back",
    )(*args)


def shards(
    hidden_in,
    counts,
    summary,
    query_weight,
    query_bias,
    key_weight,
    value_weight,
    value_bias,
    out_weight,
    out_bias,
    up_weight,
    up_bias,
    down_weight,
    down_bias,
    attn_gain,
    attn_shift,
    mlp_gain,
    mlp_shift,
    cotangent,
):
    micro_total = hidden_in.shape[0]
    rows = hidden_in.shape[1]
    groups = lax.axis_size("g")
    seq_len = rows * groups * 2
    spot = lax.axis_index(MP)
    cols = query_weight.shape[1]
    ff = up_weight.shape[1]
    micros = range(micro_total)
    quarters = range(groups)
    qk_scale = HD ** (-0.5)
    order = ring_blocks()
    back_order = jnp.argsort(order).astype(jnp.int32)
    near = 2 * rows
    core_axis = D // 2

    last = ()

    def turn(work, *args):
        nonlocal last
        args, last = lax.optimization_barrier((args, last))
        last = work(*args)
        return last

    steps = jnp.arange(rows, dtype=jnp.int32)
    place = []
    for d in quarters:
        base = spot - 2 * d
        twin = base + 1 - 2 * lax.axis_index("r")
        place += [base * rows + steps, twin * rows + steps]
    key_at = jnp.concatenate(place)
    row_at = key_at[:near]
    picker = (
        (row_at[:rows] - (seq_len - SUMM))[:, None] == jnp.arange(SUMM, dtype=jnp.int32)[None, :]
    ).astype(f32)

    join = lambda *parts: jnp.concatenate(parts)

    def by_heads(query, key, value):
        parts = [part.reshape(part.shape[:-1] + (-1, 1, 2 * HD)) for part in (query, key, value)]
        return jnp.concatenate(parts, axis=-2).reshape(query.shape[:-1] + (-1,))

    def start_rows(hidden):
        joined = hidden.astype(f32) + jnp.dot(picker, summary, precision=precise)
        normed, unit, scale = layer_norm(joined, attn_gain, attn_shift)
        return normed.astype(bf16), joined, unit, scale

    depth = query_weight.shape[0]

    def start_weights(query, key, value, out, query_add, value_add, up_add):
        adds = jnp.concatenate((by_heads(query_add, jnp.zeros_like(query_add), value_add), up_add))
        adds = jnp.concatenate((adds, jnp.zeros((64 * cols - adds.shape[0],), bf16))).reshape(16, -1)
        weights = jnp.concatenate((by_heads(query, key, value), out.T), axis=1)
        return weights, jnp.concatenate((weights, adds)), adds

    def middle_rows(joined, mine, other):
        mixed = joined + (mine + other.astype(f32)) + bias_out
        normed, unit, scale = layer_norm(mixed, mlp_gain, mlp_shift)
        return normed.astype(bf16), mixed, unit, scale

    def low_rows(left, right):
        return inner_rows(left, right).astype(bf16)

    ones = jnp.ones((cols,), f32)
    scale_qkv = by_heads(ones * qk_scale, ones, ones)
    bias_out = out_bias.astype(f32)
    bias_down = down_bias.astype(f32)

    first = [turn(start_rows, hidden_in[0])]
    near_swaps = [swap_pair(first[0][0])]
    far_shifts = [[shift_up(first[0][0], d) for d in range(1, groups)]]

    attn_own, attn_more, adds = turn(
        start_weights, query_weight, key_weight, value_weight, out_weight, query_bias, value_bias, up_bias
    )
    attn_full = [lax.all_gather(attn_own, DP, axis=0, tiled=True)]
    down_own = turn(jnp.transpose, down_weight)
    gathers = [RingGather(down_own)]
    first += [turn(start_rows, hidden_in[m]) for m in micros[1:]]

    def mark_keys(positions, used):
        return [
            jnp.where(live_keys(positions, seq_len, used[m, 0]), positions, 1 << 30).reshape(-1, 1)
            for m in micros
        ]

    key_mark = turn(mark_keys, key_at, counts)
    lows = [first[m][0] for m in micros]

    def pick_rows(values):
        picked = pick_columns(values.reshape(-1, D), order)
        return [picked[m * rows : (m + 1) * rows] for m in micros]

    cots = turn(pick_rows, cotangent)

    def first_two(mine, other, *_):
        return jnp.concatenate((mine, other))

    def split_adds(*turned):
        parts = [adds.reshape(-1)] + [part[depth:].reshape(-1) for part in turned]
        weights = [part[:depth] for part in turned]
        return weights, [part[: 3 * cols].astype(f32) for part in parts], [
            part[3 * cols : 3 * cols + ff].astype(f32) for part in parts
        ]


    def project(rows_in, weight, bias):
        return times(rows_in, weight, 0, 3 * cols, bias, scale_qkv)

    near_parts = [[None] * groups for m in micros]
    far_rows = [None] * micro_total
    far_parts = [[None] * groups for m in micros]
    logs = [[None] * groups for m in micros]
    attended = [[None] * groups for m in micros]
    out_parts = [None] * micro_total
    second = [None] * micro_total
    two_swaps = [None] * micro_total

    def near_work(m, d):
        near_parts[m][d] = turn(project, near_rows[m], attn_full[d], bias_qkv[d])

    def far_work(m, d):
        far_parts[m][d] = turn(project, far_rows[m], attn_full[d], bias_qkv[d])

    def attend_work(m, d):
        attended[m][d], logs[m][d] = turn(
            lambda n, f: attend(n, f, row_at, key_mark[m]), near_parts[m][d], far_parts[m][d]
        )

    def out_work(m):
        mine, other = turn(
            lambda *args: times_back(
                [(args[d], 0, args[groups + d], 3) for d in quarters], rows, 1, cols, 0
            ),
            *attended[m],
            *attn_full,
        )
        out_parts[m] = (mine, swap_pair(other))

    def middle_work(m):
        second[m] = turn(middle_rows, first[m][1], *out_parts[m])
        two_swaps[m] = swap_pair(second[m][0])

    bias_qkv = [adds.reshape(-1)[: 3 * cols].astype(f32)]
    near_rows = [
        turn(first_two, lows[0], near_swaps[0], *far_shifts[0], gathers[0].right, gathers[0].left)
    ]
    far_swaps = [[swap_pair(after(block, near_rows[0])) for block in far_shifts[0]]]
    attn_turned = [turn_up(after(attn_more, near_rows[0]), d) for d in range(1, groups)]
    gathers[0].advance(turn)
    near_work(0, 0)

    def far_join(m, *gate):
        blocks = [block for d in range(groups - 1) for block in (far_shifts[m][d], far_swaps[m][d])]
        count = len(blocks)
        far_rows[m] = turn(lambda *parts: jnp.concatenate(parts[:count]), *blocks, *gate)

    far_join(0, *attn_turned, gathers[0].right, gathers[0].left)
    cot_swaps = [swap_pair(after(cots[0], far_swaps[0], attn_turned))]
    for m in micros[1:]:
        low = after(lows[m], far_swaps[0], attn_turned)
        near_swaps.append(swap_pair(low))
        far_shifts.append([shift_up(low, d) for d in range(1, groups)])
    attn_shards, bias_qkv, bias_up = turn(split_adds, *attn_turned)
    attn_shards = after(attn_shards, near_parts[0][0])
    attn_full += [lax.all_gather(shard, DP, axis=0, tiled=True) for shard in attn_shards]
    far_work(0, 0)
    attend_work(0, 0)
    gathers[0].across(turn)
    for m in micros[1:]:
        near_rows.append(turn(first_two, lows[m], near_swaps[m], *far_shifts[m], cot_swaps[0]))
        far_swaps.append([swap_pair(after(block, near_rows[m])) for block in far_shifts[m]])
    up_turned = [turn_up(after(up_weight, far_swaps[-1]), d) for d in range(1, groups)]
    for d in range(1, groups):
        near_work(0, d)
        far_work(0, d)
        attend_work(0, d)
    up_full = [lax.all_gather(after(up_weight, near_parts[0][-1]), DP, axis=0, tiled=True)]
    out_work(0)
    for m in micros[1:]:
        near_work(m, 0)
    far_join(1)
    far_work(1, 0)
    attend_work(1, 0)
    down_turned = [turn_up(after(down_own, up_turned, far_parts[1][0]), d) for d in range(1, groups)]
    middle_work(0)
    cot_swaps += [swap_pair(after(cots[m], up_turned, second[0])) for m in micros[1:]]
    up_full += [lax.all_gather(after(shard, attended[1][0]), DP, axis=0, tiled=True) for shard in up_turned]
    for d in range(1, groups):
        near_work(1, d)
        far_work(1, d)
    down_full = [gathers[0].finish(turn)]
    for d in range(1, groups):
        attend_work(1, d)
    gathers += [RingGather(after(shard, attended[1][-1])) for shard in down_turned]
    out_work(1)
    cot_pair = [turn(join, cots[0], cot_swaps[0])]

    two_pair = [None] * micro_total
    held = None
    up_sums = [[None] * groups for m in micros]

    def two_work(m):
        two_pair[m] = turn(join, second[m][0], two_swaps[m])

    def hidden_units(m, d):
        nonlocal held
        *held, up_sums[m][d] = turn(
            lambda *args: expand(*args[:5], args[5:] or None, d, m, micro_total, groups),
            two_pair[m],
            cot_pair[m],
            up_full[d],
            down_full[d],
            bias_up[d],
            *(held or ()),
        )

    def back_work(m, left, weights):
        mine, other = turn(
            lambda left, *weights: times_back(
                [(left, d, weights[d], 0) for d in quarters], rows, 1, ff, m
            ),
            left,
            *weights,
        )
        return mine, other

    def middle_back(cot, mine, other, unit, scale, *_):
        grad_two = mine + other.astype(f32)
        grad_layer = cot.astype(f32)
        grad_mixed = grad_layer + norm_back(grad_two, unit, scale, mlp_gain)
        sums = jnp.stack(
            (
                jnp.sum(grad_mixed, axis=0),
                jnp.sum(grad_layer, axis=0),
                jnp.sum(grad_two * unit, axis=0),
                jnp.sum(grad_two, axis=0),
            )
        )
        return grad_mixed.astype(bf16), grad_mixed, sums

    third = [None] * micro_total
    mixed_swaps = [None] * micro_total
    mixed_pair = [None] * micro_total
    outputs = [None] * micro_total

    def third_work(m, parts, *gate):
        third[m] = turn(middle_back, cotangent[m], *parts, second[m][2], second[m][3], *gate)
        mixed_swaps[m] = swap_pair(third[m][0])

    def layer_work(m, parts):
        outputs[m] = turn(
            lambda mixed, mine, other: (
                mixed + pick_columns(mine + other.astype(f32), back_order) + bias_down
            ).astype(bf16),
            second[m][1],
            *parts,
        )

    def mixed_work(m):
        mixed_pair[m] = turn(join, third[m][0], mixed_swaps[m])

    two_work(0)
    hidden_units(0, 0)
    for gather in gathers[1:]:
        gather.advance(turn)
    middle_work(1)
    for gather in gathers[1:]:
        gather.across(turn)
    down_full += [gather.finish(turn) for gather in gathers[1:]]
    for d in range(1, groups):
        hidden_units(0, d)
    grad_first = back_work(0, held[1], up_full)
    grad_first = (grad_first[0], swap_pair(grad_first[1]))
    two_work(1)
    cot_pair += [turn(join, cots[m], cot_swaps[m]) for m in micros[1:]]
    hidden_units(1, 0)
    down_first = back_work(0, held[0], down_full)
    third_work(0, grad_first)
    for d in range(1, groups):
        hidden_units(1, d)
    grad_second = back_work(1, held[1], up_full)
    grad_second = (grad_second[0], swap_pair(grad_second[1]))
    active_all, grad_up_all = held
    down_second = back_work(1, active_all, down_full)
    mixed_work(0)
    third_work(1, grad_second)

    cot_all = turn(join, *cot_pair)
    down_other = turn(lambda left, right: low_rows(left[:, core_axis:], right), cot_all, active_all)
    down_other = swap_core(down_other)
    two_all = turn(join, *two_pair)
    up_sum = turn(low_rows, two_all, grad_up_all)
    down_first = (down_first[0], swap_pair(after(down_first[1], up_sum)))
    down_second = (down_second[0], swap_pair(after(down_second[1], up_sum)))
    up_part = lax.psum_scatter(up_sum, DP, scatter_dimension=0, tiled=True)
    down_sum = turn(
        lambda left, right, other: (
            inner_rows(left[:, :core_axis], right) + other.astype(f32)
        ).astype(bf16),
        cot_all,
        active_all,
        down_other,
    )
    down_ring = RingScatter(down_sum, down_own.shape[0])
    mixed_work(1)

    grads = None
    back_parts = [[None] * groups for m in micros]

    def grad_work(m):
        return [
            turn(lambda g, w: times(g, w, 3 * cols, cols, jnp.zeros((cols,), f32), ones), mixed_pair[m], weight)
            for weight in attn_full
        ]

    def attend_back_work(m, d, grad):
        nonlocal grads
        grads = turn(
            lambda n, f, g, l, h: attend_back(
                n, f, g, l, row_at, key_mark[m], h, d, m, micro_total, groups
            ),
            near_parts[m][d],
            far_parts[m][d],
            grad,
            logs[m][d],
            grads,
        )

    def normed_work(m, set_at):
        mine, other = turn(
            lambda left, *weights: times_back(
                [(left, d, weights[d], 0) for d in quarters], rows, 1, 3 * cols, m * groups + set_at
            ),
            grads,
            *attn_full,
        )
        back_parts[m][set_at] = (mine, swap_pair(other))

    grad = grad_work(0)
    for d in quarters:
        attend_back_work(0, d, grad[d])
    attended_all = turn(
        lambda _, __, *parts: jnp.concatenate(
            [jnp.concatenate(parts[m * groups : (m + 1) * groups], axis=1) for m in micros]
        ),
        down_first[1],
        down_second[1],
        *[part for m in micros for part in attended[m]],
    )
    mixed_all = turn(join, *mixed_pair)
    out_sum = turn(low_rows, mixed_all, attended_all)
    out_part = lax.psum_scatter(after(out_sum, up_part), DP, scatter_dimension=0, tiled=True)

    def send_parts(part, size):
        parts = turn(lambda part: [part[:, d * size : (d + 1) * size] for d in quarters], part)
        return [parts[0]] + [turn_down(parts[d], d) for d in range(1, groups)]

    def collect(parts):
        return turn(lambda *parts: sum(part.astype(f32) for part in parts), *parts)

    def far_sum(mine, other):
        return (mine + other.astype(f32)).astype(bf16)

    def last_back(grad_mixed, mine, other, unit, scale, *far):
        grad_normed = mine + other.astype(f32)
        for block in far:
            grad_normed = grad_normed + block.astype(f32)
        grad_joined = grad_mixed + norm_back(grad_normed, unit, scale, attn_gain)
        sums = jnp.stack((jnp.sum(grad_normed * unit, axis=0), jnp.sum(grad_normed, axis=0)))
        return grad_joined, sums, jnp.dot(picker.T, grad_joined, precision=precise)

    shifts = [None] * micro_total
    fourth = [None] * micro_total

    def far_back(m):
        blocks = [turn(far_sum, *back_parts[m][d]) for d in range(1, groups)]
        shifts[m] = [shift_down(blocks[d - 1], d) for d in range(1, groups)]

    def last_work(m):
        fourth[m] = turn(
            last_back, third[m][1], *back_parts[m][0], first[m][2], first[m][3], *shifts[m]
        )

    for d in range(1, groups):
        normed_work(0, d)
    normed_work(0, 0)
    far_back(0)
    grad = grad_work(1)
    attend_back_work(1, 0, grad[0])
    down_ring.advance(turn)
    up_sent = send_parts(up_part, ff)
    for d in range(1, groups):
        attend_back_work(1, d, grad[d])
    for d in range(1, groups):
        normed_work(1, d)
    normed_all = turn(
        lambda *parts: jnp.concatenate(parts),
        *[part for m in micros for part in (near_rows[m], far_rows[m])],
    )
    normed_work(1, 0)
    grad_upw = collect(up_sent)
    down_part = down_ring.finish(turn)
    qkv_sum = turn(
        low_rows, *after((normed_all, grads), out_part, shifts[0], [part[1] for part in back_parts[1][1:]])
    )

    def own_blocks(total, first_block):
        count = order.shape[0] // 2
        return jnp.concatenate(
            [
                lax.dynamic_slice_in_dim(total, order[first_block + i] * depth, depth, 0)
                for i in range(count)
            ]
        )

    qkv_other = swap_core(turn(lambda total: own_blocks(total, order.shape[0] // 2), qkv_sum))
    far_back(1)
    qkv_mine = turn(
        lambda total, other: (own_blocks(total, 0).astype(f32) + other.astype(f32)).astype(bf16),
        qkv_sum,
        qkv_other,
    )
    qkv_ring = RingScatter(qkv_mine, depth)
    held_sum = turn(lambda grads: jnp.sum(grads.astype(f32), axis=0), grads)
    layer_work(0, down_first)
    qkv_ring.advance(turn)
    down_sent = send_parts(down_part, ff)
    last_work(0)
    layer_work(1, down_second)
    last_work(1)
    input_grads = [fourth[m][0] for m in micros]

    held_sum = held_sum.reshape(groups, -1, 3, 2 * HD)
    parts = jnp.concatenate(
        (
            held_sum[:, :, 0].reshape(groups, cols),
            held_sum[:, :, 2].reshape(groups, cols),
            jnp.concatenate([sum(up_sums[m][d] for m in micros) for d in quarters]),
        ),
        axis=1,
    )
    places = jnp.arange(2 * groups, dtype=jnp.int32)
    slots = jnp.zeros((2 * groups, parts.shape[1]), f32)
    for d in quarters:
        slots = slots + jnp.where(
            places[:, None] == (spot - 2 * d) % (2 * groups), parts[d][None], 0.0
        )
    small = jnp.concatenate(
        (
            sum(third[m][2] for m in micros),
            sum(fourth[m][1] for m in micros),
            sum(fourth[m][2] for m in micros),
            slots.reshape(-1, D),
        )
    )
    small = turn(
        lambda small: jnp.concatenate((small, jnp.zeros((-small.shape[0] % 16, D), f32))), small
    )
    summing = SumAll(small, turn)
    qkv_part = qkv_ring.finish(turn)
    qkv_sent = send_parts(qkv_part, 3 * cols)
    out_sent = send_parts(out_part, cols)
    while summing.left > 1:
        summing.advance(turn)
    grad_down = collect(down_sent).T
    small = summing.finish(turn)
    row_total = [small[i] for i in (0, 1, 4, 5, 2, 3)] + [small[6 : 6 + SUMM]]
    slots = small[6 + SUMM : 6 + SUMM + slots.size // D].reshape(slots.shape)
    bias_grad = lax.dynamic_index_in_dim(slots, spot, 0, keepdims=False)
    grad_out = collect(out_sent).T
    grad_qkv = collect(qkv_sent)
    grad_qkv = grad_qkv.reshape(grad_qkv.shape[0], -1, 3, 2 * HD)
    grad_query, grad_key, grad_value = (grad_qkv[:, :, i].reshape(-1, cols) for i in range(3))
    return (
        jnp.stack(outputs),
        jnp.stack(input_grads),
        row_total[6],
        grad_query,
        bias_grad[:cols],
        grad_key,
        grad_value,
        bias_grad[cols : 2 * cols],
        grad_out,
        row_total[0],
        grad_upw,
        bias_grad[2 * cols :],
        grad_down,
        row_total[1],
        row_total[2],
        row_total[3],
        row_total[4],
        row_total[5],
    )


def solution(mesh):
    data = mesh.shape["dp"]
    model = mesh.shape["mp"]
    fine = Mesh(mesh.devices.reshape(data // 2, 2, model // 2, 2), ALL)
    rows_spec = P(None, ALL, None)
    wide_spec = P(DP, MP)
    tall_spec = P(MP, DP)
    in_specs = (
        rows_spec,
        P(None, DP),
        P(),
        wide_spec,
        P(MP),
        wide_spec,
        wide_spec,
        P(MP),
        tall_spec,
        P(),
        wide_spec,
        P(MP),
        tall_spec,
        P(),
        P(),
        P(),
        P(),
        P(),
        rows_spec,
    )
    out_specs = (
        rows_spec,
        rows_spec,
        P(),
        wide_spec,
        P(MP),
        wide_spec,
        wide_spec,
        P(MP),
        tall_spec,
        P(),
        wide_spec,
        P(MP),
        tall_spec,
        P(),
        P(),
        P(),
        P(),
        P(),
    )
    return jax.shard_map(shards, mesh=fine, in_specs=in_specs, out_specs=out_specs, check_vma=False)
```

time: 2060 us -> 1080 us (0.52)
  waiting for transfers between devices: 1260 us -> 277 us
  matrix products: 513 us -> 97.3 us
  Pallas kernels: 0 us -> 346 us
  local copies, waits for them, and re-layouts: 56.1 us -> 143 us
  starting transfers between devices: 2.06 us -> 77.7 us
  blocking collectives: 64 us -> 0 us
    all_gather x14 -> x4, waiting for transfers between devices: 596 us -> 1.53 us  [the longest x1 1.53 us: shards(): attn_full = [lax.all_gather(attn_own, DP, axis=0, tiled=True)]]
    reduce_scatter x14 -> x2, waiting for transfers between devices: 581 us -> 0.01 us  [the longest x1 0.01 us: shards(): up_part = lax.psum_scatter(up_sum, DP, scatter_dimension=0, tiled=True)]
    dot_general x55 -> x3, matrix products: 415 us -> 3.97 us  [the longest x2 2.72 us: last_back(): jnp.dot(picker.T, grad_joined, precision=precise)]
    pallas_call x0 -> x37, Pallas kernels: none -> 346 us  [the longest x10 115 us: times_back(): pl.pallas_call(functools.partial(back_kernel, len(parts), rows), grid=(wi...]
    ppermute x0 -> x57, waiting for transfers between devices: none -> 276 us  [the longest x20 161 us: swap_pair(): return lax.ppermute(values, 'r', [(0, 1), (1, 0)])]
    psum x1 -> x0, waiting for transfers between devices: 81.9 us -> none  [shards(): lax.psum((row_sums[0], row_sums[1], row_sums[2], row_sums[3], row_sums[4]...]
    ppermute x0 -> x57, starting transfers between devices: none -> 76.8 us  [the longest x20 21.5 us: swap_pair(): return lax.ppermute(values, 'r', [(0, 1), (1, 0)])]
    psum x2 -> x0, blocking collectives: 64 us -> none  [the longest x1 41.8 us: shards(): lax.psum((row_sums[0], row_sums[1], row_sums[2], row_sums[3], row_sums[4]...]
  transfers between devices with their start and end apart: 29 -> 63, of which waited for: 23 -> 30; matrix products, arithmetic and copies ran while one was open for 31% -> 18% of each run, Pallas kernels for 0% -> 32%
where the time goes in v1:
time: 1080 us; the launch traced here: 1070 us
  Pallas kernels  346 us (32%)
  waiting for transfers between devices  277 us (26%)
  local copies, waits for them, and re-layouts  143 us (13%)
  other arithmetic  107 us (10%)
  matrix products  97.3 us (9%)
  starting transfers between devices  77.7 us (7%)
  between operations  21.9 us (2%)
    ppermute x20, waiting for transfers between devices, swap_pair(): return lax.ppermute(values, 'r', [(0, 1), (1, 0)])  161 us
    pallas_call x10, Pallas kernels, times_back(): pl.pallas_call(functools.partial(back_kernel, len(parts), rows), grid=(wi...  115 us
    dot_general x5, matrix products, inner_rows(): lax.dot_general(left_side, right_side, (((0,), (0,)), ((), ())), preferre...  93.4 us
    unnamed x329, local copies, waits for them, and re-layouts  74.2 us
    pallas_call x4, Pallas kernels, attend_back(): pl.pallas_call(attend_back_kernel, grid=(pairs,), in_specs=in_specs, out_...  65.3 us
    pallas_call x12, Pallas kernels, times(): pl.pallas_call(times_kernel, grid=(columns // block,), in_specs=[pl.Block...  59.8 us
    ppermute x4, waiting for transfers between devices, turn_down(): lax.ppermute(values, 'g', [((i + step) % size, i) for i in range(size)])  52.4 us
    pallas_call x4, Pallas kernels, expand(): pl.pallas_call(expand_kernel, grid=(count,), in_specs=in_specs, out_specs...  50.8 us
  transfers between devices with their start and end apart: 63, of which 30 were waited for; matrix products, arithmetic and copies ran while one was open for 18% of the time, Pallas kernels for 32%

profile of v1, /device:TPU:1, one launch (start us, length us, event | category | flops | bytes accessed | tf_op | source)
XLA Modules:
  0.0 1069.6 jit_solution(2463272221174225207)
XLA Ops:
  61.0 13.2 %collective-permute-done = bf16[256,2048]{1,0:T(8,128)(2,1)} collective-permute-done((bf16[256,2048]{1,0:T(8,128)(2,1)}, bf16[256,2048]{1,0:T(8,128)(2,1)}, u32[]{:S(2)}, u32[]{:S(2)}) %collective-permute-start) | collective-permute-done | bytes 1048608 | tf_op jit(solution)/shard_map/ppermute | solution.py:72
  99.0 21.5 %collective-permute-done.4 = bf16[256,2048]{1,0:T(8,128)(2,1)S(1)} collective-permute-done((bf16[256,2048]{1,0:T(8,128)(2,1)}, bf16[256,2048]{1,0:T(8,128)(2,1)S(1)}, u32[]{:S(2)}, u32[]{:S(2)}) %collective-permute-start.4) | collective-permute-done | bytes 1048608 | tf_op jit(solution)/shard_map/ppermute | solution.py:72
  160.2 36.4 %collective-permute-done.10 = bf16[256,2048]{1,0:T(8,128)(2,1)S(1)} collective-permute-done((bf16[256,2048]{1,0:T(8,128)(2,1)}, bf16[256,2048]{1,0:T(8,128)(2,1)S(1)}, u32[]{:S(2)}, u32[]{:S(2)}) %collective-permute-start.10) | collective-permute-done | bytes 1048608 | tf_op jit(solution)/shard_map/ppermute | solution.py:72
  212.3 17.2 %collective-permute-done.12 = bf16[256,2048]{1,0:T(8,128)(2,1)} collective-permute-done((bf16[256,2048]{1,0:T(8,128)(2,1)}, bf16[256,2048]{1,0:T(8,128)(2,1)}, u32[]{:S(2)}, u32[]{:S(2)}) %collective-permute-start.12) | collective-permute-done | bytes 1048608 | tf_op jit(solution)/shard_map/ppermute | solution.py:72
  284.4 41.9 %collective-permute-done.11 = bf16[256,2048]{1,0:T(8,128)(2,1)S(1)} collective-permute-done((bf16[256,2048]{1,0:T(8,128)(2,1)}, bf16[256,2048]{1,0:T(8,128)(2,1)S(1)}, u32[]{:S(2)}, u32[]{:S(2)}) %collective-permute-start.11) | collective-permute-done | bytes 1048608 | tf_op jit(solution)/shard_map/ppermute | solution.py:72
  378.0 12.8 %expand.4 = (bf16[1024,4096]{1,0:T(8,128)(2,1)}, bf16[1024,4096]{1,0:T(8,128)(2,1)}, f32[1,2048]{1,0:T(1,128)S(1)}) custom-call(bf16[512,2048]{1,0:T(8,128)(2,1)S(1)} %copy-done.22, bf16[512,2048]{1,0:T(8,128)(2,1)S(1)} %copy-done.18, bf16[2048,2048]{1,0:T(8,128)(2,1)} %all-gather.9.cloned.1.call-done.up_ref.refs_1_, ...), custom_call_target="tpu_custom_call" | custom-call | flops 8589934592 | bytes 16777216 | tf_op jit(solution)/shard_map/expand/pallas_call | solution.py:389
  427.6 12.7 %expand.5 = (bf16[1024,4096]{1,0:T(8,128)(2,1)}, bf16[1024,4096]{1,0:T(8,128)(2,1)}, f32[1,2048]{1,0:T(1,128)S(1)}) custom-call(bf16[512,2048]{1,0:T(8,128)(2,1)S(1)} %copy-done.23, bf16[512,2048]{1,0:T(8,128)(2,1)S(1)} %copy-done.19, bf16[2048,2048]{1,0:T(8,128)(2,1)} %all-gather.11.cloned.1.call-done.up_ref.refs_3_, ...), custom_call_target="tpu_custom_call", output_to_operand_aliasing={{0}: (5, {}), {1}: (6, {})} | custom-call | flops 8589934592 | bytes 16777216 | tf_op jit(solution)/shard_map/expand/pallas_call | solution.py:389
  440.4 13.9 %times_back.12 = (f32[256,2048]{1,0:T(8,128)}, bf16[256,2048]{1,0:T(8,128)(2,1)}) custom-call(bf16[1024,4096]{1,0:T(8,128)(2,1)} %get-tuple-element.495.refs_0_.refs_2_.rest_1_, bf16[2048,2048]{1,0:T(8,128)(2,1)} %all-gather.9.cloned.1.call-done.up_ref.refs_1_, bf16[1024,4096]{1,0:T(8,128)(2,1)} %get-tuple-element.495.refs_0_.refs_2_.rest_1_, ...), custom_call_target="tpu_custom_call" | custom-call | flops 8589934592 | bytes 16777216 | tf_op jit(solution)/shard_map/times_back/pallas_call | solution.py:451
  467.0 12.6 %expand.6 = (bf16[1024,4096]{1,0:T(8,128)(2,1)}, bf16[1024,4096]{1,0:T(8,128)(2,1)}, f32[1,2048]{1,0:T(1,128)S(1)}) custom-call(bf16[512,2048]{1,0:T(8,128)(2,1)S(1)} %constant_dynamic-update-slice_fusion.26.two_ref, bf16[512,2048]{1,0:T(8,128)(2,1)S(1)} %constant_dynamic-update-slice_fusion.28.cot_ref, ...), custom_call_target="tpu_custom_call", output_to_operand_aliasing={{0}: (5, {}), {1}: (6, {})} | custom-call | flops 8589934592 | bytes 16777216 | tf_op jit(solution)/shard_map/expand/pallas_call | solution.py:389
  479.7 13.9 %times_back.13 = (f32[256,2048]{1,0:T(8,128)}, bf16[256,2048]{1,0:T(8,128)(2,1)}) custom-call(bf16[1024,4096]{1,0:T(8,128)(2,1)} %get-tuple-element.514.refs_0_.refs_2_.rest_0_, bf16[2048,2048]{1,0:T(8,128)(2,1)} %constant_dynamic-update-slice_fusion.13.down_ref.refs_1_, bf16[1024,4096]{1,0:T(8,128)(2,1)} %get-tuple-element.514.refs_0_.refs_2_.rest_0_, ...), custom_call_target="tpu_custom_call" | custom-call | flops 8589934592 | bytes 16777216 | tf_op jit(solution)/shard_map/times_back/pallas_call | solution.py:451
  502.9 12.7 %expand.7 = (bf16[1024,4096]{1,0:T(8,128)(2,1)}, bf16[1024,4096]{1,0:T(8,128)(2,1)}, f32[1,2048]{1,0:T(1,128)S(1)}) custom-call(bf16[512,2048]{1,0:T(8,128)(2,1)S(1)} %constant_dynamic-update-slice_fusion.26.two_ref, bf16[512,2048]{1,0:T(8,128)(2,1)S(1)} %constant_dynamic-update-slice_fusion.28.cot_ref, ...), custom_call_target="tpu_custom_call", output_to_operand_aliasing={{0}: (5, {}), {1}: (6, {})} | custom-call | flops 8589934592 | bytes 16777216 | tf_op jit(solution)/shard_map/expand/pallas_call | solution.py:389
  515.6 14.1 %times_back.14 = (f32[256,2048]{1,0:T(8,128)}, bf16[256,2048]{1,0:T(8,128)(2,1)}) custom-call(bf16[1024,4096]{1,0:T(8,128)(2,1)} %get-tuple-element.543.refs_0_.refs_2_, bf16[2048,2048]{1,0:T(8,128)(2,1)} %all-gather.9.cloned.1.call-done.up_ref.refs_1_, bf16[1024,4096]{1,0:T(8,128)(2,1)} %get-tuple-element.543.refs_0_.refs_2_, ...), custom_call_target="tpu_custom_call" | custom-call | flops 8589934592 | bytes 16777216 | tf_op jit(solution)/shard_map/times_back/pallas_call | solution.py:451
  530.1 13.9 %times_back.15 = (f32[256,2048]{1,0:T(8,128)}, bf16[256,2048]{1,0:T(8,128)(2,1)}) custom-call(bf16[1024,4096]{1,0:T(8,128)(2,1)} %get-tuple-element.546.refs_0_.refs_2_, bf16[2048,2048]{1,0:T(8,128)(2,1)} %constant_dynamic-update-slice_fusion.13.down_ref.refs_1_, bf16[1024,4096]{1,0:T(8,128)(2,1)} %get-tuple-element.546.refs_0_.refs_2_, ...), custom_call_target="tpu_custom_call" | custom-call | flops 8589934592 | bytes 16777216 | tf_op jit(solution)/shard_map/times_back/pallas_call | solution.py:451
  576.1 25.0 %convolution_convert_fusion = bf16[2048,4096]{1,0:T(8,128)(2,1)} fusion(bf16[1024,2048]{1,0:T(8,128)(2,1)} %pad_maximum_fusion.1, bf16[1024,4096]{1,0:T(8,128)(2,1)} %get-tuple-element.543.refs_0_.refs_2_), kind=kOutput, calls=%fused_computation.3 | convolution fusion | flops 17188257792 | bytes 29360128 | tf_op jit(solution)/shard_map/dot_general | solution.py:59
  617.4 18.8 %add_convert_fusion = bf16[1024,4096]{1,0:T(8,128)(2,1)} fusion(bf16[1024,4096]{1,0:T(8,128)(2,1)} %collective-permute-done.30, bf16[1024,4096]{1,0:T(8,128)(2,1)} %get-tuple-element.546.refs_0_.refs_2_, bf16[1024,2048]{1,0:T(8,128)(2,1)} %copy-done.105), kind=kOutput, calls=%fused_computation.2 | convolution fusion | flops 8602517504 | bytes 27262976 | tf_op jit(solution)/shard_map/dot_general | solution.py:59
  644.8 16.2 %attend_back.4.rest_0_ = bf16[2048,3072]{1,0:T(8,128)(2,1)} custom-call(s32[1,512]{1,0:T(1,128)S(1)} %bitcast.109, s32[1024,1]{1,0:T(8,128)S(1)} %copy.63.key_ref, bf16[512,1536]{1,0:T(8,128)(2,1)S(1)} %copy-done.35, bf16[512,1536]{1,0:T(8,128)(2,1)S(1)} %copy-done.37, bf16[512,512]{1,0:T(8,128)(2,1)S(1)} %times.20.grad_ref, ...), custom_call_target="tpu_custom_call" | custom-call | flops 17179869184 | bytes 9437184 | tf_op jit(solution)/shard_map/attend_back/pallas_call | solution.py:348
  662.5 16.4 %attend_back.5.refs_0_.refs_2_.rest_0_ = bf16[2048,3072]{1,0:T(8,128)(2,1)} custom-call(s32[1,512]{1,0:T(1,128)S(1)} %bitcast.110, s32[1024,1]{1,0:T(8,128)S(1)} %copy.63.key_ref, bf16[512,1536]{1,0:T(8,128)(2,1)S(1)} %copy-done.48, bf16[512,1536]{1,0:T(8,128)(2,1)S(1)} %copy-done.50, ...), custom_call_target="tpu_custom_call", output_to_operand_aliasing={{}: (6, {})} | custom-call | flops 17179869184 | bytes 9437184 | tf_op jit(solution)/shard_map/attend_back/pallas_call | solution.py:348
  732.6 16.6 %attend_back.6.rest_0_ = bf16[2048,3072]{1,0:T(8,128)(2,1)} custom-call(s32[1,512]{1,0:T(1,128)S(1)} %bitcast.111, s32[1024,1]{1,0:T(8,128)S(1)} %copy-done.52, bf16[512,1536]{1,0:T(8,128)(2,1)S(1)} %copy-done.39, bf16[512,1536]{1,0:T(8,128)(2,1)S(1)} %copy-done.43, bf16[512,512]{1,0:T(8,128)(2,1)S(1)} %times.22.grad_ref, ...), custom_call_target="tpu_custom_call", output_to_operand_aliasing={{}: (6, {})} | custom-call | flops 17179869184 | bytes 9437184 | tf_op jit(solution)/shard_map/attend_back/pallas_call | solution.py:348
  765.3 16.1 %attend_back.7.refs_0_.refs_2_ = bf16[2048,3072]{1,0:T(8,128)(2,1)} custom-call(s32[1,512]{1,0:T(1,128)S(1)} %bitcast.112, s32[1024,1]{1,0:T(8,128)S(1)} %copy-done.52, bf16[512,1536]{1,0:T(8,128)(2,1)S(1)} %copy-done.41, bf16[512,1536]{1,0:T(8,128)(2,1)S(1)} %copy-done.45, bf16[512,512]{1,0:T(8,128)(2,1)S(1)} %times.23.grad_ref, ...), custom_call_target="tpu_custom_call", output_to_operand_aliasing={{}: (6, {})} | custom-call | flops 17179869184 | bytes 9437184 | tf_op jit(solution)/shard_map/attend_back/pallas_call | solution.py:348
  781.4 12.0 %times_back.18 = (f32[256,2048]{1,0:T(8,128)}, bf16[256,2048]{1,0:T(8,128)(2,1)}) custom-call(bf16[2048,3072]{1,0:T(8,128)(2,1)} %attend_back.7.refs_0_.refs_2_, bf16[2048,2048]{1,0:T(8,128)(2,1)} %all-gather.5.cloned.1.call-done.w_ref.refs_1_, bf16[2048,3072]{1,0:T(8,128)(2,1)} %attend_back.7.refs_0_.refs_2_, ...), custom_call_target="tpu_custom_call" | custom-call | flops 6442450944 | bytes 12582912 | tf_op jit(solution)/shard_map/times_back/pallas_call | solution.py:451
  827.6 16.2 %collective-permute-done.36 = bf16[256,2048]{1,0:T(8,128)(2,1)S(1)} collective-permute-done((bf16[256,2048]{1,0:T(8,128)(2,1)}, bf16[256,2048]{1,0:T(8,128)(2,1)S(1)}, u32[]{:S(2)}, u32[]{:S(2)}) %collective-permute-start.36) | collective-permute-done | bytes 1048608 | tf_op jit(solution)/shard_map/ppermute | solution.py:72
  843.7 32.1 %convolution_convert_fusion.1 = bf16[2048,3072]{1,0:T(8,128)(2,1)S(1)} fusion(bf16[2048,2048]{1,0:T(8,128)(2,1)} %constant_dynamic-update-slice_fusion.36, bf16[2048,3072]{1,0:T(8,128)(2,1)} %attend_back.7.refs_0_.refs_2_), kind=kOutput, calls=%fused_computation.5 | convolution fusion | flops 25776095232 | bytes 33554432 | tf_op jit(solution)/shard_map/dot_general | solution.py:59
  990.5 26.9 %collective-permute-done.52 = bf16[256,2048]{1,0:T(8,128)(2,1)} collective-permute-done((bf16[256,2048]{1,0:T(8,128)(2,1)}, bf16[256,2048]{1,0:T(8,128)(2,1)}, u32[]{:S(2)}, u32[]{:S(2)}) %collective-permute-start.52) | collective-permute-done | bytes 1048608 | tf_op jit(solution)/shard_map/ppermute | solution.py:96
  1020.9 19.0 %collective-permute-done.55 = bf16[256,1536]{1,0:T(8,128)(2,1)} collective-permute-done((bf16[256,1536]{1,0:T(8,128)(2,1)}, bf16[256,1536]{1,0:T(8,128)(2,1)}, u32[]{:S(2)}, u32[]{:S(2)}) %collective-permute-start.55) | collective-permute-done | bytes 786464 | tf_op jit(solution)/shard_map/ppermute | solution.py:96
  (664 shorter events, 595.5 us)
Async XLA Ops:
  7.2 81.1 %all-gather.5.cloned.1.call-start = ((), (), s32[]{:S(2)}) async-start(), calls=%async_computation.2 | async-start | bytes 9437184 | tf_op jit(solution)/shard_map/all_gather | solution.py:563
  19.9 179.4 %all-gather.7.cloned.1.call-start = ((), (), s32[]{:S(2)}) async-start(), calls=%async_computation.3 | async-start | bytes 9437184 | tf_op jit(solution)/shard_map/all_gather | solution.py:653
  129.8 244.9 %all-gather.9.cloned.1.call-start = ((), (), s32[]{:S(2)}) async-start(), calls=%async_computation.4 | async-start | bytes 9437184 | tf_op jit(solution)/shard_map/all_gather | solution.py:665
  130.2 66.5 %collective-permute-start.8 = (bf16[256,2048]{1,0:T(8,128)(2,1)}, bf16[256,2048]{1,0:T(8,128)(2,1)S(1)}, u32[]{:S(2)}, u32[]{:S(2)}) collective-permute-start(bf16[256,2048]{1,0:T(8,128)(2,1)} %get-tuple-element.388), channel_id=1, source_target_pairs={{0,1},{1,0},{2,3},{3,2},{4,5},{5,4},{6,7},{7,6},{8,9},{9,8},{10,11... | collective-permute-start | bytes 3145736 | tf_op jit(solution)/shard_map/ppermute | solution.py:72
  130.9 65.7 %collective-permute-start.9 = (bf16[256,2048]{1,0:T(8,128)(2,1)}, bf16[256,2048]{1,0:T(8,128)(2,1)S(1)}, u32[]{:S(2)}, u32[]{:S(2)}) collective-permute-start(bf16[256,2048]{1,0:T(8,128)(2,1)} %get-tuple-element.388), channel_id=1, source_target_pairs={{0,2},{1,3},{4,6},{5,7},{8,10},{9,11},{12,14},{13,15},{16,18},{17,... | collective-permute-start | bytes 3145736 | tf_op jit(solution)/shard_map/ppermute | solution.py:81
  137.0 59.7 %collective-permute-start.10 = (bf16[256,2048]{1,0:T(8,128)(2,1)}, bf16[256,2048]{1,0:T(8,128)(2,1)S(1)}, u32[]{:S(2)}, u32[]{:S(2)}) collective-permute-start(bf16[256,2048]{1,0:T(8,128)(2,1)} %get-tuple-element.443), channel_id=1, source_target_pairs={{0,1},{1,0},{2,3},{3,2},{4,5},{5,4},{6,7},{7,6},{8,9},{9,8},{10,11... | collective-permute-start | bytes 3145736 | tf_op jit(solution)/shard_map/ppermute | solution.py:72
  206.3 218.2 %all-gather.11.cloned.1.call-start = ((), (), s32[]{:S(2)}) async-start(), calls=%async_computation.5 | async-start | bytes 9437184 | tf_op jit(solution)/shard_map/all_gather | solution.py:675
  208.9 135.4 %collective-permute-start.13 = (bf16[1024,2048]{1,0:T(8,128)(2,1)}, bf16[1024,2048]{1,0:T(8,128)(2,1)}, u32[]{:S(2)}, u32[]{:S(2)}) collective-permute-start(bf16[1024,2048]{1,0:T(8,128)(2,1)} %copy-done.81), channel_id=1, source_target_pairs={{0,4},{4,0},{1,5},{5,1},{2,6},{6,2},{3,7},{7,3},{8,12},{12,8},{9,1... | collective-permute-start | bytes 12582920 | tf_op jit(solution)/shard_map/ppermute | solution.py:76
  229.5 52.8 %collective-permute-start.15 = (bf16[256,2048]{1,0:T(8,128)(2,1)}, bf16[256,2048]{1,0:T(8,128)(2,1)}, u32[]{:S(2)}, u32[]{:S(2)}) collective-permute-start(bf16[256,2048]{1,0:T(8,128)(2,1)} %param.32), channel_id=1, source_target_pairs={{0,2},{2,0},{1,3},{3,1},{4,6},{6,4},{5,7},{7,5},{8,10},{10,8},{9,1... | collective-permute-start | bytes 3145736 | tf_op jit(solution)/shard_map/ppermute | solution.py:91
  282.3 473.7 %reduce-scatter.3.cloned.1.call-start = ((), (), s32[]{:S(2)}) async-start(), calls=%async_computation.6 | async-start | bytes 18874368 | tf_op jit(solution)/shard_map/reduce_scatter | solution.py:783
  284.0 77.4 %collective-permute-start.16 = (bf16[256,2048]{1,0:T(8,128)(2,1)}, bf16[256,2048]{1,0:T(8,128)(2,1)}, u32[]{:S(2)}, u32[]{:S(2)}) collective-permute-start(bf16[256,2048]{1,0:T(8,128)(2,1)} %bitcast.121), channel_id=1, source_target_pairs={{0,2},{2,0},{1,3},{3,1},{4,6},{6,4},{5,7},{7,5},{8,10},{10,8},{9,1... | collective-permute-start | bytes 3145736 | tf_op jit(solution)/shard_map/ppermute | solution.py:91
  601.2 242.6 %reduce-scatter.5.cloned.1.call-start = ((), (), s32[]{:S(2)}) async-start(), calls=%async_computation.7 | async-start | bytes 4718592 | tf_op jit(solution)/shard_map/reduce_scatter | solution.py:840
  607.9 70.9 %collective-permute-start.28 = (bf16[256,2048]{1,0:T(8,128)(2,1)}, bf16[256,2048]{1,0:T(8,128)(2,1)S(1)}, u32[]{:S(2)}, u32[]{:S(2)}) collective-permute-start(bf16[256,2048]{1,0:T(8,128)(2,1)} %get-tuple-element.544), channel_id=1, source_target_pairs={{0,1},{1,0},{2,3},{3,2},{4,5},{5,4},{6,7},{7,6},{8,9},{9,8},{10,11... | collective-permute-start | bytes 3145736 | tf_op jit(solution)/shard_map/ppermute | solution.py:72
  609.1 69.8 %collective-permute-start.31 = (bf16[256,2048]{1,0:T(8,128)(2,1)}, bf16[256,2048]{1,0:T(8,128)(2,1)S(1)}, u32[]{:S(2)}, u32[]{:S(2)}) collective-permute-start(bf16[256,2048]{1,0:T(8,128)(2,1)} %get-tuple-element.563), channel_id=1, source_target_pairs={{0,1},{1,0},{2,3},{3,2},{4,5},{5,4},{6,7},{7,6},{8,9},{9,8},{10,11... | collective-permute-start | bytes 3145736 | tf_op jit(solution)/shard_map/ppermute | solution.py:72
  725.3 102.3 %collective-permute-start.35 = (bf16[256,2048]{1,0:T(8,128)(2,1)}, bf16[256,2048]{1,0:T(8,128)(2,1)}, u32[]{:S(2)}, u32[]{:S(2)}) collective-permute-start(bf16[256,2048]{1,0:T(8,128)(2,1)} %add_convert_fusion.9), channel_id=1, source_target_pairs={{2,0},{3,1},{6,4},{7,5},{10,8},{11,9},{14,12},{15,13},{18,16},{19,... | collective-permute-start | bytes 3145736 | tf_op jit(solution)/shard_map/ppermute | solution.py:86
  753.3 69.0 %collective-permute-start.38 = (bf16[256,4096]{1,0:T(8,128)(2,1)}, bf16[256,4096]{1,0:T(8,128)(2,1)}, u32[]{:S(2)}, u32[]{:S(2)}) collective-permute-start(bf16[256,4096]{1,0:T(8,128)(2,1)} %pad_maximum_fusion.5), channel_id=1, source_target_pairs={{0,16},{8,0},{24,8},{16,24},{1,17},{9,1},{25,9},{17,25},{2,18},{10... | collective-permute-start | bytes 6291464 | tf_op jit(solution)/shard_map/ppermute | solution.py:115
  759.3 63.0 %collective-permute-start.37 = (bf16[256,4096]{1,0:T(8,128)(2,1)}, bf16[256,4096]{1,0:T(8,128)(2,1)}, u32[]{:S(2)}, u32[]{:S(2)}) collective-permute-start(bf16[256,4096]{1,0:T(8,128)(2,1)} %pad_maximum_fusion.4), channel_id=1, source_target_pairs={{0,8},{8,24},{24,16},{16,0},{1,9},{9,25},{25,17},{17,1},{2,10},{10... | collective-permute-start | bytes 6291464 | tf_op jit(solution)/shard_map/ppermute | solution.py:115
  760.7 59.9 %collective-permute-start.39 = (bf16[256,2048]{1,0:T(8,128)(2,1)S(1)}, bf16[256,2048]{1,0:T(8,128)(2,1)S(1)}, u32[]{:S(2)}, u32[]{:S(2)}) collective-permute-start(bf16[256,2048]{1,0:T(8,128)(2,1)S(1)} %get-tuple-element.776), channel_id=1, source_target_pairs={{2,0},{0,2},{3,1},{1,3},{6,4},{4,6},{7,5},{5,7},{10,8},{8,10},{11,... | collective-permute-start | bytes 3145736 | tf_op jit(solution)/shard_map/ppermute | solution.py:96
  888.1 54.4 %collective-permute-start.41 = (bf16[256,2048]{1,0:T(8,128)(2,1)}, bf16[256,2048]{1,0:T(8,128)(2,1)}, u32[]{:S(2)}, u32[]{:S(2)}) collective-permute-start(bf16[256,2048]{1,0:T(8,128)(2,1)} %get-tuple-element.581), channel_id=1, source_target_pairs={{0,1},{1,0},{2,3},{3,2},{4,5},{5,4},{6,7},{7,6},{8,9},{9,8},{10,11... | collective-permute-start | bytes 3145736 | tf_op jit(solution)/shard_map/ppermute | solution.py:72
  888.1 72.1 %collective-permute-start.44 = (bf16[256,2048]{1,0:T(8,128)(2,1)}, bf16[256,2048]{1,0:T(8,128)(2,1)}, u32[]{:S(2)}, u32[]{:S(2)}) collective-permute-start(bf16[256,2048]{1,0:T(8,128)(2,1)} %get-tuple-element.619), channel_id=1, source_target_pairs={{0,1},{1,0},{2,3},{3,2},{4,5},{5,4},{6,7},{7,6},{8,9},{9,8},{10,11... | collective-permute-start | bytes 3145736 | tf_op jit(solution)/shard_map/ppermute | solution.py:72
  890.9 69.3 %collective-permute-start.45 = (bf16[256,2048]{1,0:T(8,128)(2,1)}, bf16[256,2048]{1,0:T(8,128)(2,1)}, u32[]{:S(2)}, u32[]{:S(2)}) collective-permute-start(bf16[256,2048]{1,0:T(8,128)(2,1)} %add_convert_fusion.6), channel_id=1, source_target_pairs={{2,0},{3,1},{6,4},{7,5},{10,8},{11,9},{14,12},{15,13},{18,16},{19,... | collective-permute-start | bytes 3145736 | tf_op jit(solution)/shard_map/ppermute | solution.py:86
  942.4 75.0 %collective-permute-start.52 = (bf16[256,2048]{1,0:T(8,128)(2,1)}, bf16[256,2048]{1,0:T(8,128)(2,1)}, u32[]{:S(2)}, u32[]{:S(2)}) collective-permute-start(bf16[256,2048]{1,0:T(8,128)(2,1)} %get-tuple-element.774), channel_id=1, source_target_pairs={{2,0},{0,2},{3,1},{1,3},{6,4},{4,6},{7,5},{5,7},{10,8},{8,10},{11,... | collective-permute-start | bytes 3145736 | tf_op jit(solution)/shard_map/ppermute | solution.py:96
  982.6 57.3 %collective-permute-start.55 = (bf16[256,1536]{1,0:T(8,128)(2,1)}, bf16[256,1536]{1,0:T(8,128)(2,1)}, u32[]{:S(2)}, u32[]{:S(2)}) collective-permute-start(bf16[256,1536]{1,0:T(8,128)(2,1)} %get-tuple-element.787), channel_id=1, source_target_pairs={{2,0},{0,2},{3,1},{1,3},{6,4},{4,6},{7,5},{5,7},{10,8},{8,10},{11,... | collective-permute-start | bytes 2359304 | tf_op jit(solution)/shard_map/ppermute | solution.py:96
  986.7 72.2 %collective-permute-start.56 = (bf16[256,512]{1,0:T(8,128)(2,1)}, bf16[256,512]{1,0:T(8,128)(2,1)}, u32[]{:S(2)}, u32[]{:S(2)}) collective-permute-start(bf16[256,512]{1,0:T(8,128)(2,1)} %get-tuple-element.797), channel_id=1, source_target_pairs={{2,0},{0,2},{3,1},{1,3},{6,4},{4,6},{7,5},{5,7},{10,8},{8,10},{11,... | collective-permute-start | bytes 786440 | tf_op jit(solution)/shard_map/ppermute | solution.py:96
  (187 other events, 2377.5 us)
Sparse Core Ops, SparseCore 0:
  20.0 68.2 all-gather.4
  130.0 58.4 all-gather.6
  206.4 60.9 all-gather.8
  282.4 57.4 all-gather.10
  601.3 146.0 reduce-scatter.2
  756.1 68.9 reduce-scatter.4

commit v2 on v1

--- a/solution.py
+++ b/solution.py
@@ -643,7 +643,6 @@
         far_rows[m] = turn(lambda *parts: jnp.concatenate(parts[:count]), *blocks, *gate)
 
     far_join(0, *attn_turned, gathers[0].right, gathers[0].left)
-    cot_swaps = [swap_pair(after(cots[0], far_swaps[0], attn_turned))]
     for m in micros[1:]:
         low = after(lows[m], far_swaps[0], attn_turned)
         near_swaps.append(swap_pair(low))
@@ -655,9 +654,10 @@
     attend_work(0, 0)
     gathers[0].across(turn)
     for m in micros[1:]:
-        near_rows.append(turn(first_two, lows[m], near_swaps[m], *far_shifts[m], cot_swaps[0]))
+        near_rows.append(turn(first_two, lows[m], near_swaps[m], *far_shifts[m]))
         far_swaps.append([swap_pair(after(block, near_rows[m])) for block in far_shifts[m]])
     up_turned = [turn_up(after(up_weight, far_swaps[-1]), d) for d in range(1, groups)]
+    cot_swaps = [swap_pair(after(cots[0], far_swaps[-1]))]
     for d in range(1, groups):
         near_work(0, d)
         far_work(0, d)
@@ -672,14 +672,16 @@
     down_turned = [turn_up(after(down_own, up_turned, far_parts[1][0]), d) for d in range(1, groups)]
     middle_work(0)
     cot_swaps += [swap_pair(after(cots[m], up_turned, second[0])) for m in micros[1:]]
-    up_full += [lax.all_gather(after(shard, attended[1][0]), DP, axis=0, tiled=True) for shard in up_turned]
     for d in range(1, groups):
         near_work(1, d)
         far_work(1, d)
+    up_full += [
+        lax.all_gather(after(shard, near_parts[1][-1]), DP, axis=0, tiled=True) for shard in up_turned
+    ]
+    gathers += [RingGather(shard) for shard in down_turned]
     down_full = [gathers[0].finish(turn)]
     for d in range(1, groups):
         attend_work(1, d)
-    gathers += [RingGather(after(shard, attended[1][-1])) for shard in down_turned]
     out_work(1)
     cot_pair = [turn(join, cots[0], cot_swaps[0])]
 

time: 1080 us -> 1080 us (level)
    ppermute x20, waiting for transfers between devices: 161 us -> 138 us  [swap_pair(): return lax.ppermute(values, 'r', [(0, 1), (1, 0)])]
    ppermute x2, waiting for transfers between devices: 0.01 us -> 14.1 us  [shift_up(): lax.ppermute(values, 'g', [(i, i + step) for i in range(size - step)])]
    all_gather x1, waiting for transfers between devices: 0.01 us -> 11.9 us  [shards(): lax.all_gather(shard, DP, axis=0, tiled=True)]
    unnamed x329 -> x327, local copies, waits for them, and re-layouts: 74.2 us -> 71.9 us
  transfers between devices with their start and end apart: 63 -> 63, of which waited for: 30 -> 33; matrix products, arithmetic and copies ran while one was open for 18% -> 18% of each run, Pallas kernels for 32% -> 32%
where the time goes in v2:
time: 1080 us; the launch traced here: 1070 us
  Pallas kernels  347 us (32%)
  waiting for transfers between devices  280 us (26%)
  local copies, waits for them, and re-layouts  141 us (13%)
  other arithmetic  109 us (10%)
  matrix products  97.4 us (9%)
  starting transfers between devices  72.3 us (7%)
  between operations  21.9 us (2%)
    ppermute x20, waiting for transfers between devices, swap_pair(): return lax.ppermute(values, 'r', [(0, 1), (1, 0)])  138 us
    pallas_call x10, Pallas kernels, times_back(): pl.pallas_call(functools.partial(back_kernel, len(parts), rows), grid=(wi...  115 us
    dot_general x5, matrix products, inner_rows(): lax.dot_general(left_side, right_side, (((0,), (0,)), ((), ())), preferre...  93.4 us
    unnamed x327, local copies, waits for them, and re-layouts  71.9 us
    pallas_call x4, Pallas kernels, attend_back(): pl.pallas_call(attend_back_kernel, grid=(pairs,), in_specs=in_specs, out_...  65.1 us
    pallas_call x12, Pallas kernels, times(): pl.pallas_call(times_kernel, grid=(columns // block,), in_specs=[pl.Block...  60.4 us
    ppermute x4, waiting for transfers between devices, turn_down(): lax.ppermute(values, 'g', [((i + step) % size, i) for i in range(size)])  50.8 us
    pallas_call x4, Pallas kernels, expand(): pl.pallas_call(expand_kernel, grid=(count,), in_specs=in_specs, out_specs...  50.8 us
  transfers between devices with their start and end apart: 63, of which 33 were waited for; matrix products, arithmetic and copies ran while one was open for 18% of the time, Pallas kernels for 32%

profile of v2, /device:TPU:1, one launch (start us, length us, event | category | flops | bytes accessed | tf_op | source)
XLA Modules:
  0.0 1068.0 jit_solution(10264428308099605718)
XLA Ops:
  60.4 13.2 %collective-permute-done = bf16[256,2048]{1,0:T(8,128)(2,1)} collective-permute-done((bf16[256,2048]{1,0:T(8,128)(2,1)}, bf16[256,2048]{1,0:T(8,128)(2,1)}, u32[]{:S(2)}, u32[]{:S(2)}) %collective-permute-start) | collective-permute-done | bytes 1048608 | tf_op jit(solution)/shard_map/ppermute | solution.py:72
  98.4 21.5 %collective-permute-done.4 = bf16[256,2048]{1,0:T(8,128)(2,1)S(1)} collective-permute-done((bf16[256,2048]{1,0:T(8,128)(2,1)}, bf16[256,2048]{1,0:T(8,128)(2,1)S(1)}, u32[]{:S(2)}, u32[]{:S(2)}) %collective-permute-start.4) | collective-permute-done | bytes 1048608 | tf_op jit(solution)/shard_map/ppermute | solution.py:72
  159.5 14.1 %collective-permute-done.9 = bf16[256,2048]{1,0:T(8,128)(2,1)S(1)} collective-permute-done((bf16[256,2048]{1,0:T(8,128)(2,1)}, bf16[256,2048]{1,0:T(8,128)(2,1)S(1)}, u32[]{:S(2)}, u32[]{:S(2)}) %collective-permute-start.9) | collective-permute-done | bytes 1048608 | tf_op jit(solution)/shard_map/ppermute | solution.py:81
  197.3 22.8 %collective-permute-done.11 = bf16[256,2048]{1,0:T(8,128)(2,1)} collective-permute-done((bf16[256,2048]{1,0:T(8,128)(2,1)}, bf16[256,2048]{1,0:T(8,128)(2,1)}, u32[]{:S(2)}, u32[]{:S(2)}) %collective-permute-start.11) | collective-permute-done | bytes 1048608 | tf_op jit(solution)/shard_map/ppermute | solution.py:72
  270.8 20.3 %collective-permute-done.10 = bf16[256,2048]{1,0:T(8,128)(2,1)S(1)} collective-permute-done((bf16[256,2048]{1,0:T(8,128)(2,1)}, bf16[256,2048]{1,0:T(8,128)(2,1)S(1)}, u32[]{:S(2)}, u32[]{:S(2)}) %collective-permute-start.10) | collective-permute-done | bytes 1048608 | tf_op jit(solution)/shard_map/ppermute | solution.py:72
  353.6 19.6 %collective-permute-done.18 = bf16[256,2048]{1,0:T(8,128)(2,1)S(1)} collective-permute-done((bf16[256,2048]{1,0:T(8,128)(2,1)}, bf16[256,2048]{1,0:T(8,128)(2,1)S(1)}, u32[]{:S(2)}, u32[]{:S(2)}) %collective-permute-start.18) | collective-permute-done | bytes 1048608 | tf_op jit(solution)/shard_map/ppermute | solution.py:72
  378.0 12.8 %expand.4 = (bf16[1024,4096]{1,0:T(8,128)(2,1)}, bf16[1024,4096]{1,0:T(8,128)(2,1)}, f32[1,2048]{1,0:T(1,128)S(1)}) custom-call(bf16[512,2048]{1,0:T(8,128)(2,1)S(1)} %copy-done.21, bf16[512,2048]{1,0:T(8,128)(2,1)S(1)} %copy-done.17, bf16[2048,2048]{1,0:T(8,128)(2,1)} %all-gather.9.cloned.1.call-done.up_ref.refs_1_, ...), custom_call_target="tpu_custom_call" | custom-call | flops 8589934592 | bytes 16777216 | tf_op jit(solution)/shard_map/expand/pallas_call | solution.py:389
  427.6 12.8 %expand.5 = (bf16[1024,4096]{1,0:T(8,128)(2,1)}, bf16[1024,4096]{1,0:T(8,128)(2,1)}, f32[1,2048]{1,0:T(1,128)S(1)}) custom-call(bf16[512,2048]{1,0:T(8,128)(2,1)S(1)} %copy-done.22, bf16[512,2048]{1,0:T(8,128)(2,1)S(1)} %copy-done.18, bf16[2048,2048]{1,0:T(8,128)(2,1)} %all-gather.11.cloned.1.call-done.up_ref.refs_3_, ...), custom_call_target="tpu_custom_call", output_to_operand_aliasing={{0}: (5, {}), {1}: (6, {})} | custom-call | flops 8589934592 | bytes 16777216 | tf_op jit(solution)/shard_map/expand/pallas_call | solution.py:389
  440.3 13.9 %times_back.12 = (f32[256,2048]{1,0:T(8,128)}, bf16[256,2048]{1,0:T(8,128)(2,1)}) custom-call(bf16[1024,4096]{1,0:T(8,128)(2,1)} %get-tuple-element.493.refs_0_.refs_2_.rest_1_, bf16[2048,2048]{1,0:T(8,128)(2,1)} %all-gather.9.cloned.1.call-done.up_ref.refs_1_, bf16[1024,4096]{1,0:T(8,128)(2,1)} %get-tuple-element.493.refs_0_.refs_2_.rest_1_, ...), custom_call_target="tpu_custom_call" | custom-call | flops 8589934592 | bytes 16777216 | tf_op jit(solution)/shard_map/times_back/pallas_call | solution.py:451
  466.9 12.6 %expand.6 = (bf16[1024,4096]{1,0:T(8,128)(2,1)}, bf16[1024,4096]{1,0:T(8,128)(2,1)}, f32[1,2048]{1,0:T(1,128)S(1)}) custom-call(bf16[512,2048]{1,0:T(8,128)(2,1)S(1)} %constant_dynamic-update-slice_fusion.26.two_ref, bf16[512,2048]{1,0:T(8,128)(2,1)S(1)} %constant_dynamic-update-slice_fusion.28.cot_ref, ...), custom_call_target="tpu_custom_call", output_to_operand_aliasing={{0}: (5, {}), {1}: (6, {})} | custom-call | flops 8589934592 | bytes 16777216 | tf_op jit(solution)/shard_map/expand/pallas_call | solution.py:389
  479.5 13.9 %times_back.13 = (f32[256,2048]{1,0:T(8,128)}, bf16[256,2048]{1,0:T(8,128)(2,1)}) custom-call(bf16[1024,4096]{1,0:T(8,128)(2,1)} %get-tuple-element.512.refs_0_.refs_2_.rest_0_, bf16[2048,2048]{1,0:T(8,128)(2,1)} %constant_dynamic-update-slice_fusion.13.down_ref.refs_1_, bf16[1024,4096]{1,0:T(8,128)(2,1)} %get-tuple-element.512.refs_0_.refs_2_.rest_0_, ...), custom_call_target="tpu_custom_call" | custom-call | flops 8589934592 | bytes 16777216 | tf_op jit(solution)/shard_map/times_back/pallas_call | solution.py:451
  502.1 12.6 %expand.7 = (bf16[1024,4096]{1,0:T(8,128)(2,1)}, bf16[1024,4096]{1,0:T(8,128)(2,1)}, f32[1,2048]{1,0:T(1,128)S(1)}) custom-call(bf16[512,2048]{1,0:T(8,128)(2,1)S(1)} %constant_dynamic-update-slice_fusion.26.two_ref, bf16[512,2048]{1,0:T(8,128)(2,1)S(1)} %constant_dynamic-update-slice_fusion.28.cot_ref, ...), custom_call_target="tpu_custom_call", output_to_operand_aliasing={{0}: (5, {}), {1}: (6, {})} | custom-call | flops 8589934592 | bytes 16777216 | tf_op jit(solution)/shard_map/expand/pallas_call | solution.py:389
  514.7 14.1 %times_back.14 = (f32[256,2048]{1,0:T(8,128)}, bf16[256,2048]{1,0:T(8,128)(2,1)}) custom-call(bf16[1024,4096]{1,0:T(8,128)(2,1)} %get-tuple-element.541.refs_0_.refs_2_, bf16[2048,2048]{1,0:T(8,128)(2,1)} %all-gather.9.cloned.1.call-done.up_ref.refs_1_, bf16[1024,4096]{1,0:T(8,128)(2,1)} %get-tuple-element.541.refs_0_.refs_2_, ...), custom_call_target="tpu_custom_call" | custom-call | flops 8589934592 | bytes 16777216 | tf_op jit(solution)/shard_map/times_back/pallas_call | solution.py:451
  529.9 13.9 %times_back.15 = (f32[256,2048]{1,0:T(8,128)}, bf16[256,2048]{1,0:T(8,128)(2,1)}) custom-call(bf16[1024,4096]{1,0:T(8,128)(2,1)} %get-tuple-element.544.refs_0_.refs_2_, bf16[2048,2048]{1,0:T(8,128)(2,1)} %constant_dynamic-update-slice_fusion.13.down_ref.refs_1_, bf16[1024,4096]{1,0:T(8,128)(2,1)} %get-tuple-element.544.refs_0_.refs_2_, ...), custom_call_target="tpu_custom_call" | custom-call | flops 8589934592 | bytes 16777216 | tf_op jit(solution)/shard_map/times_back/pallas_call | solution.py:451
  575.1 25.1 %convolution_convert_fusion = bf16[2048,4096]{1,0:T(8,128)(2,1)} fusion(bf16[1024,2048]{1,0:T(8,128)(2,1)} %pad_maximum_fusion.1, bf16[1024,4096]{1,0:T(8,128)(2,1)} %get-tuple-element.541.refs_0_.refs_2_), kind=kOutput, calls=%fused_computation.3 | convolution fusion | flops 17188257792 | bytes 29360128 | tf_op jit(solution)/shard_map/dot_general | solution.py:59
  616.5 18.7 %add_convert_fusion = bf16[1024,4096]{1,0:T(8,128)(2,1)} fusion(bf16[1024,4096]{1,0:T(8,128)(2,1)} %collective-permute-done.30, bf16[1024,4096]{1,0:T(8,128)(2,1)} %get-tuple-element.544.refs_0_.refs_2_, bf16[1024,2048]{1,0:T(8,128)(2,1)} %copy-done.106), kind=kOutput, calls=%fused_computation.2 | convolution fusion | flops 8602517504 | bytes 27262976 | tf_op jit(solution)/shard_map/dot_general | solution.py:59
  643.9 16.2 %attend_back.4.rest_0_ = bf16[2048,3072]{1,0:T(8,128)(2,1)} custom-call(s32[1,512]{1,0:T(1,128)S(1)} %bitcast.109, s32[1024,1]{1,0:T(8,128)S(1)} %copy.63.key_ref, bf16[512,1536]{1,0:T(8,128)(2,1)S(1)} %copy-done.34, bf16[512,1536]{1,0:T(8,128)(2,1)S(1)} %copy-done.39, bf16[512,512]{1,0:T(8,128)(2,1)S(1)} %times.20.grad_ref, ...), custom_call_target="tpu_custom_call" | custom-call | flops 17179869184 | bytes 9437184 | tf_op jit(solution)/shard_map/attend_back/pallas_call | solution.py:348
  661.5 16.3 %attend_back.5.refs_0_.refs_2_.rest_0_ = bf16[2048,3072]{1,0:T(8,128)(2,1)} custom-call(s32[1,512]{1,0:T(1,128)S(1)} %bitcast.110, s32[1024,1]{1,0:T(8,128)S(1)} %copy.63.key_ref, bf16[512,1536]{1,0:T(8,128)(2,1)S(1)} %copy-done.48, bf16[512,1536]{1,0:T(8,128)(2,1)S(1)} %copy-done.50, ...), custom_call_target="tpu_custom_call", output_to_operand_aliasing={{}: (6, {})} | custom-call | flops 17179869184 | bytes 9437184 | tf_op jit(solution)/shard_map/attend_back/pallas_call | solution.py:348
  731.3 16.6 %attend_back.6.rest_0_ = bf16[2048,3072]{1,0:T(8,128)(2,1)} custom-call(s32[1,512]{1,0:T(1,128)S(1)} %bitcast.111, s32[1024,1]{1,0:T(8,128)S(1)} %copy-done.52, bf16[512,1536]{1,0:T(8,128)(2,1)S(1)} %copy-done.41, bf16[512,1536]{1,0:T(8,128)(2,1)S(1)} %copy-done.43, bf16[512,512]{1,0:T(8,128)(2,1)S(1)} %times.22.grad_ref, ...), custom_call_target="tpu_custom_call", output_to_operand_aliasing={{}: (6, {})} | custom-call | flops 17179869184 | bytes 9437184 | tf_op jit(solution)/shard_map/attend_back/pallas_call | solution.py:348
  763.5 16.1 %attend_back.7.refs_0_.refs_2_ = bf16[2048,3072]{1,0:T(8,128)(2,1)} custom-call(s32[1,512]{1,0:T(1,128)S(1)} %bitcast.112, s32[1024,1]{1,0:T(8,128)S(1)} %copy-done.52, bf16[512,1536]{1,0:T(8,128)(2,1)S(1)} %copy-done.37, bf16[512,1536]{1,0:T(8,128)(2,1)S(1)} %copy-done.45, bf16[512,512]{1,0:T(8,128)(2,1)S(1)} %times.23.grad_ref, ...), custom_call_target="tpu_custom_call", output_to_operand_aliasing={{}: (6, {})} | custom-call | flops 17179869184 | bytes 9437184 | tf_op jit(solution)/shard_map/attend_back/pallas_call | solution.py:348
  825.8 16.3 %collective-permute-done.36 = bf16[256,2048]{1,0:T(8,128)(2,1)S(1)} collective-permute-done((bf16[256,2048]{1,0:T(8,128)(2,1)}, bf16[256,2048]{1,0:T(8,128)(2,1)S(1)}, u32[]{:S(2)}, u32[]{:S(2)}) %collective-permute-start.36) | collective-permute-done | bytes 1048608 | tf_op jit(solution)/shard_map/ppermute | solution.py:72
  842.1 32.2 %convolution_convert_fusion.1 = bf16[2048,3072]{1,0:T(8,128)(2,1)S(1)} fusion(bf16[2048,2048]{1,0:T(8,128)(2,1)} %constant_dynamic-update-slice_fusion.36, bf16[2048,3072]{1,0:T(8,128)(2,1)} %attend_back.7.refs_0_.refs_2_), kind=kOutput, calls=%fused_computation.5 | convolution fusion | flops 25776095232 | bytes 33554432 | tf_op jit(solution)/shard_map/dot_general | solution.py:59
  990.2 25.6 %collective-permute-done.52 = bf16[256,2048]{1,0:T(8,128)(2,1)} collective-permute-done((bf16[256,2048]{1,0:T(8,128)(2,1)}, bf16[256,2048]{1,0:T(8,128)(2,1)}, u32[]{:S(2)}, u32[]{:S(2)}) %collective-permute-start.52) | collective-permute-done | bytes 1048608 | tf_op jit(solution)/shard_map/ppermute | solution.py:96
  1019.3 19.0 %collective-permute-done.55 = bf16[256,1536]{1,0:T(8,128)(2,1)} collective-permute-done((bf16[256,1536]{1,0:T(8,128)(2,1)}, bf16[256,1536]{1,0:T(8,128)(2,1)}, u32[]{:S(2)}, u32[]{:S(2)}) %collective-permute-start.55) | collective-permute-done | bytes 786464 | tf_op jit(solution)/shard_map/ppermute | solution.py:96
  (662 shorter events, 625.9 us)
Async XLA Ops:
  7.2 80.6 %all-gather.5.cloned.1.call-start = ((), (), s32[]{:S(2)}) async-start(), calls=%async_computation.2 | async-start | bytes 9437184 | tf_op jit(solution)/shard_map/all_gather | solution.py:563
  19.4 168.5 %all-gather.7.cloned.1.call-start = ((), (), s32[]{:S(2)}) async-start(), calls=%async_computation.3 | async-start | bytes 9437184 | tf_op jit(solution)/shard_map/all_gather | solution.py:652
  129.3 245.5 %all-gather.9.cloned.1.call-start = ((), (), s32[]{:S(2)}) async-start(), calls=%async_computation.4 | async-start | bytes 9437184 | tf_op jit(solution)/shard_map/all_gather | solution.py:665
  194.9 229.5 %all-gather.11.cloned.1.call-start = ((), (), s32[]{:S(2)}) async-start(), calls=%async_computation.5 | async-start | bytes 9437184 | tf_op jit(solution)/shard_map/all_gather | solution.py:679
  196.7 118.6 %collective-permute-start.12 = (bf16[1024,2048]{1,0:T(8,128)(2,1)}, bf16[1024,2048]{1,0:T(8,128)(2,1)}, u32[]{:S(2)}, u32[]{:S(2)}) collective-permute-start(bf16[1024,2048]{1,0:T(8,128)(2,1)} %copy-done.81), channel_id=1, source_target_pairs={{0,4},{4,0},{1,5},{5,1},{2,6},{6,2},{3,7},{7,3},{8,12},{12,8},{9,1... | collective-permute-start | bytes 12582920 | tf_op jit(solution)/shard_map/ppermute | solution.py:76
  220.0 83.1 %collective-permute-start.14 = (bf16[256,2048]{1,0:T(8,128)(2,1)}, bf16[256,2048]{1,0:T(8,128)(2,1)}, u32[]{:S(2)}, u32[]{:S(2)}) collective-permute-start(bf16[256,2048]{1,0:T(8,128)(2,1)} %param.32), channel_id=1, source_target_pairs={{0,2},{2,0},{1,3},{3,1},{4,6},{6,4},{5,7},{7,5},{8,10},{10,8},{9,1... | collective-permute-start | bytes 3145736 | tf_op jit(solution)/shard_map/ppermute | solution.py:91
  303.2 451.6 %reduce-scatter.3.cloned.1.call-start = ((), (), s32[]{:S(2)}) async-start(), calls=%async_computation.6 | async-start | bytes 18874368 | tf_op jit(solution)/shard_map/reduce_scatter | solution.py:785
  307.0 66.2 %collective-permute-start.18 = (bf16[256,2048]{1,0:T(8,128)(2,1)}, bf16[256,2048]{1,0:T(8,128)(2,1)S(1)}, u32[]{:S(2)}, u32[]{:S(2)}) collective-permute-start(bf16[256,2048]{1,0:T(8,128)(2,1)} %get-tuple-element.443), channel_id=1, source_target_pairs={{0,1},{1,0},{2,3},{3,2},{4,5},{5,4},{6,7},{7,6},{8,9},{9,8},{10,11... | collective-permute-start | bytes 3145736 | tf_op jit(solution)/shard_map/ppermute | solution.py:72
  338.6 57.0 %collective-permute-start.13 = (bf16[256,2048]{1,0:T(8,128)(2,1)}, bf16[256,2048]{1,0:T(8,128)(2,1)}, u32[]{:S(2)}, u32[]{:S(2)}) collective-permute-start(bf16[256,2048]{1,0:T(8,128)(2,1)} %get-tuple-element.437), channel_id=1, source_target_pairs={{0,1},{1,0},{2,3},{3,2},{4,5},{5,4},{6,7},{7,6},{8,9},{9,8},{10,11... | collective-permute-start | bytes 3145736 | tf_op jit(solution)/shard_map/ppermute | solution.py:72
  414.3 49.9 %collective-permute-start.24 = (bf16[256,2048]{1,0:T(8,128)(2,1)}, bf16[256,2048]{1,0:T(8,128)(2,1)}, u32[]{:S(2)}, u32[]{:S(2)}) collective-permute-start(bf16[256,2048]{1,0:T(8,128)(2,1)} %get-tuple-element.485), channel_id=1, source_target_pairs={{0,1},{1,0},{2,3},{3,2},{4,5},{5,4},{6,7},{7,6},{8,9},{9,8},{10,11... | collective-permute-start | bytes 3145736 | tf_op jit(solution)/shard_map/ppermute | solution.py:72
  600.2 241.9 %reduce-scatter.5.cloned.1.call-start = ((), (), s32[]{:S(2)}) async-start(), calls=%async_computation.7 | async-start | bytes 4718592 | tf_op jit(solution)/shard_map/reduce_scatter | solution.py:842
  607.8 70.0 %collective-permute-start.28 = (bf16[256,2048]{1,0:T(8,128)(2,1)}, bf16[256,2048]{1,0:T(8,128)(2,1)S(1)}, u32[]{:S(2)}, u32[]{:S(2)}) collective-permute-start(bf16[256,2048]{1,0:T(8,128)(2,1)} %get-tuple-element.542), channel_id=1, source_target_pairs={{0,1},{1,0},{2,3},{3,2},{4,5},{5,4},{6,7},{7,6},{8,9},{9,8},{10,11... | collective-permute-start | bytes 3145736 | tf_op jit(solution)/shard_map/ppermute | solution.py:72
  608.2 69.6 %collective-permute-start.31 = (bf16[256,2048]{1,0:T(8,128)(2,1)}, bf16[256,2048]{1,0:T(8,128)(2,1)S(1)}, u32[]{:S(2)}, u32[]{:S(2)}) collective-permute-start(bf16[256,2048]{1,0:T(8,128)(2,1)} %get-tuple-element.561), channel_id=1, source_target_pairs={{0,1},{1,0},{2,3},{3,2},{4,5},{5,4},{6,7},{7,6},{8,9},{9,8},{10,11... | collective-permute-start | bytes 3145736 | tf_op jit(solution)/shard_map/ppermute | solution.py:72
  724.1 101.6 %collective-permute-start.35 = (bf16[256,2048]{1,0:T(8,128)(2,1)}, bf16[256,2048]{1,0:T(8,128)(2,1)}, u32[]{:S(2)}, u32[]{:S(2)}) collective-permute-start(bf16[256,2048]{1,0:T(8,128)(2,1)} %add_convert_fusion.9), channel_id=1, source_target_pairs={{2,0},{3,1},{6,4},{7,5},{10,8},{11,9},{14,12},{15,13},{18,16},{19,... | collective-permute-start | bytes 3145736 | tf_op jit(solution)/shard_map/ppermute | solution.py:86
  752.0 68.5 %collective-permute-start.38 = (bf16[256,4096]{1,0:T(8,128)(2,1)}, bf16[256,4096]{1,0:T(8,128)(2,1)}, u32[]{:S(2)}, u32[]{:S(2)}) collective-permute-start(bf16[256,4096]{1,0:T(8,128)(2,1)} %pad_maximum_fusion.5), channel_id=1, source_target_pairs={{0,16},{8,0},{24,8},{16,24},{1,17},{9,1},{25,9},{17,25},{2,18},{10... | collective-permute-start | bytes 6291464 | tf_op jit(solution)/shard_map/ppermute | solution.py:115
  758.1 62.4 %collective-permute-start.37 = (bf16[256,4096]{1,0:T(8,128)(2,1)}, bf16[256,4096]{1,0:T(8,128)(2,1)}, u32[]{:S(2)}, u32[]{:S(2)}) collective-permute-start(bf16[256,4096]{1,0:T(8,128)(2,1)} %pad_maximum_fusion.4), channel_id=1, source_target_pairs={{0,8},{8,24},{24,16},{16,0},{1,9},{9,25},{25,17},{17,1},{2,10},{10... | collective-permute-start | bytes 6291464 | tf_op jit(solution)/shard_map/ppermute | solution.py:115
  759.5 59.3 %collective-permute-start.39 = (bf16[256,2048]{1,0:T(8,128)(2,1)S(1)}, bf16[256,2048]{1,0:T(8,128)(2,1)S(1)}, u32[]{:S(2)}, u32[]{:S(2)}) collective-permute-start(bf16[256,2048]{1,0:T(8,128)(2,1)S(1)} %get-tuple-element.774), channel_id=1, source_target_pairs={{2,0},{0,2},{3,1},{1,3},{6,4},{4,6},{7,5},{5,7},{10,8},{8,10},{11,... | collective-permute-start | bytes 3145736 | tf_op jit(solution)/shard_map/ppermute | solution.py:96
  791.6 50.5 %collective-permute-start.36 = (bf16[256,2048]{1,0:T(8,128)(2,1)}, bf16[256,2048]{1,0:T(8,128)(2,1)S(1)}, u32[]{:S(2)}, u32[]{:S(2)}) collective-permute-start(bf16[256,2048]{1,0:T(8,128)(2,1)} %get-tuple-element.605), channel_id=1, source_target_pairs={{0,1},{1,0},{2,3},{3,2},{4,5},{5,4},{6,7},{7,6},{8,9},{9,8},{10,11... | collective-permute-start | bytes 3145736 | tf_op jit(solution)/shard_map/ppermute | solution.py:72
  886.3 54.9 %collective-permute-start.41 = (bf16[256,2048]{1,0:T(8,128)(2,1)}, bf16[256,2048]{1,0:T(8,128)(2,1)}, u32[]{:S(2)}, u32[]{:S(2)}) collective-permute-start(bf16[256,2048]{1,0:T(8,128)(2,1)} %get-tuple-element.579), channel_id=1, source_target_pairs={{0,1},{1,0},{2,3},{3,2},{4,5},{5,4},{6,7},{7,6},{8,9},{9,8},{10,11... | collective-permute-start | bytes 3145736 | tf_op jit(solution)/shard_map/ppermute | solution.py:72
  886.4 72.5 %collective-permute-start.44 = (bf16[256,2048]{1,0:T(8,128)(2,1)}, bf16[256,2048]{1,0:T(8,128)(2,1)}, u32[]{:S(2)}, u32[]{:S(2)}) collective-permute-start(bf16[256,2048]{1,0:T(8,128)(2,1)} %get-tuple-element.617), channel_id=1, source_target_pairs={{0,1},{1,0},{2,3},{3,2},{4,5},{5,4},{6,7},{7,6},{8,9},{9,8},{10,11... | collective-permute-start | bytes 3145736 | tf_op jit(solution)/shard_map/ppermute | solution.py:72
  889.1 69.8 %collective-permute-start.45 = (bf16[256,2048]{1,0:T(8,128)(2,1)}, bf16[256,2048]{1,0:T(8,128)(2,1)}, u32[]{:S(2)}, u32[]{:S(2)}) collective-permute-start(bf16[256,2048]{1,0:T(8,128)(2,1)} %add_convert_fusion.6), channel_id=1, source_target_pairs={{2,0},{3,1},{6,4},{7,5},{10,8},{11,9},{14,12},{15,13},{18,16},{19,... | collective-permute-start | bytes 3145736 | tf_op jit(solution)/shard_map/ppermute | solution.py:86
  941.2 74.6 %collective-permute-start.52 = (bf16[256,2048]{1,0:T(8,128)(2,1)}, bf16[256,2048]{1,0:T(8,128)(2,1)}, u32[]{:S(2)}, u32[]{:S(2)}) collective-permute-start(bf16[256,2048]{1,0:T(8,128)(2,1)} %get-tuple-element.772), channel_id=1, source_target_pairs={{2,0},{0,2},{3,1},{1,3},{6,4},{4,6},{7,5},{5,7},{10,8},{8,10},{11,... | collective-permute-start | bytes 3145736 | tf_op jit(solution)/shard_map/ppermute | solution.py:96
  981.4 56.8 %collective-permute-start.55 = (bf16[256,1536]{1,0:T(8,128)(2,1)}, bf16[256,1536]{1,0:T(8,128)(2,1)}, u32[]{:S(2)}, u32[]{:S(2)}) collective-permute-start(bf16[256,1536]{1,0:T(8,128)(2,1)} %get-tuple-element.785), channel_id=1, source_target_pairs={{2,0},{0,2},{3,1},{1,3},{6,4},{4,6},{7,5},{5,7},{10,8},{8,10},{11,... | collective-permute-start | bytes 2359304 | tf_op jit(solution)/shard_map/ppermute | solution.py:96
  986.2 71.1 %collective-permute-start.56 = (bf16[256,512]{1,0:T(8,128)(2,1)}, bf16[256,512]{1,0:T(8,128)(2,1)}, u32[]{:S(2)}, u32[]{:S(2)}) collective-permute-start(bf16[256,512]{1,0:T(8,128)(2,1)} %get-tuple-element.795), channel_id=1, source_target_pairs={{2,0},{0,2},{3,1},{1,3},{6,4},{4,6},{7,5},{5,7},{10,8},{8,10},{11,... | collective-permute-start | bytes 786440 | tf_op jit(solution)/shard_map/ppermute | solution.py:96
  (186 other events, 2374.1 us)
Sparse Core Ops, SparseCore 0:
  19.5 68.2 all-gather.4
  129.4 58.4 all-gather.6
  195.0 54.3 all-gather.8
  303.3 55.9 all-gather.10
  600.4 141.5 reduce-scatter.2
  754.9 68.9 reduce-scatter.4
